TPU v7x, 32 devices: a whole 2x2x4 slice. The times are simulated.
32 devices in a mesh: seq: 8 (over z, y), head: 4 (over x, core).
Axes of the slice: x: 2, y: 2, z: 4, core: 2. Of those that a mesh axis runs over, the one named last changes fastest.
Arguments:
- queries: bfloat16 [4096, 4096], P(('seq', 'head')), may hold values from -6 to 6
- keys: bfloat16 [4096, 2, 4096], P(('seq', 'head')), may hold values from -6 to 6
- values: bfloat16 [4096, 2, 4096], P(('seq', 'head')), may hold values from -6 to 6
- betas: bfloat16 [4096, 2, 16], P(('seq', 'head')), may hold values from 0.2 to 2, as said below
- gate: bfloat16 [4096, 4096], P(('seq', 'head')), may hold values from -6 to 6
- norm_gain: float32 [256], replicated, may hold values from 0.1 to 1.9
Outputs:
- mixed: bfloat16 [4096, 4096], P(('seq', 'head'))
Inputs may be any that keep to these rules, and one draw needn't show every extreme that they name: `betas`: each entry is the step size of one reflection of one head.
All inputs are finite; a program needn't handle non-finite values.
Results may differ from a plain program's by a relative error of at most 0.0049.
Values may be sent and summed in bfloat16 or wider, within the bound.
No kernel may reach another device: no remote copies, remote signals or barrier semaphores. Data moves between devices by JAX's collectives and lax.ppermute only.
A program may use at most 128 MiB of HBM per device.

v0:
```python
import jax
import jax.numpy as jnp
from jax import lax
from jax.sharding import PartitionSpec as P

REFL = 2
CT = 128


epsilon = 1e-06
highest = lax.Precision.HIGHEST


def shifted(block, axis, distance):
    devices = range(lax.axis_size(axis))
    route = [(i - distance, i) for i in devices if i - distance in devices]
    return lax.ppermute(block, axis, route)


def unit_rows(matrix):
    return matrix / jnp.sqrt(jnp.sum(matrix * matrix, axis=-1, keepdims=True) + epsilon)


def matmul_heads(left_side, right_side):
    return jnp.einsum("hde,hef->hdf", left_side, right_side, precision=highest)


def combine_pairs(earlier, later):
    return (matmul_heads(later[0], earlier[0]), matmul_heads(later[0], earlier[1]) + later[1])


def block_factors(key_parts, value_parts, beta_parts):
    seq_rows = key_parts.shape[0]
    local_heads = key_parts.shape[2]
    width_per_head = key_parts.shape[3]
    blocks = seq_rows // CT
    block_steps = CT * REFL
    k_unit = unit_rows(key_parts.astype(jnp.float32))
    k_blocks = (
        k_unit.reshape(blocks, CT, REFL, local_heads, width_per_head)
        .transpose(0, 3, 1, 2, 4)
        .reshape(blocks, local_heads, block_steps, width_per_head)
    )
    v_blocks = (
        value_parts.astype(jnp.float32)
        .reshape(blocks, CT, REFL, local_heads, width_per_head)
        .transpose(0, 3, 1, 2, 4)
        .reshape(blocks, local_heads, block_steps, width_per_head)
    )
    b_blocks = (
        beta_parts.astype(jnp.float32)
        .reshape(blocks, CT, REFL, local_heads)
        .transpose(0, 3, 1, 2)
        .reshape(blocks, local_heads, block_steps)
    )
    gram_rows = jnp.einsum("chid,chjd->chij", k_blocks, k_blocks, precision=highest)
    lower_part = jnp.tril(gram_rows, -1) * b_blocks[:, :, None, :]
    solved = lax.linalg.triangular_solve(
        lower_part,
        jnp.concatenate([k_blocks, v_blocks], axis=-1),
        left_side=True,
        lower=True,
        unit_diagonal=True,
    )
    w_rows = solved[..., :width_per_head] * b_blocks[..., None]
    y_rows = solved[..., width_per_head:] * b_blocks[..., None]
    identity = jnp.eye(width_per_head, dtype=jnp.float32)
    trans_a = identity - jnp.einsum("chid,chie->chde", k_blocks, w_rows, precision=highest)
    trans_b = jnp.einsum("chid,chie->chde", k_blocks, y_rows, precision=highest)
    return (k_blocks, w_rows, y_rows, trans_a, trans_b)


def shards(queries, keys, values, betas, gate, norm_gain):
    tok_rows = queries.shape[0]
    width_per_head = norm_gain.shape[0]
    head_count = queries.shape[1] // width_per_head
    query_parts = queries.reshape(tok_rows, 1, head_count, width_per_head)
    key_parts = keys.reshape(tok_rows, REFL, head_count, width_per_head)
    value_parts = values.reshape(tok_rows, REFL, head_count, width_per_head)
    beta_parts = betas.reshape(tok_rows, REFL, head_count, 1)
    query_parts, key_parts, value_parts, beta_parts = (
        lax.all_to_all(query_parts, "head", split_axis=2, concat_axis=0, tiled=True),
        lax.all_to_all(key_parts, "head", split_axis=2, concat_axis=0, tiled=True),
        lax.all_to_all(value_parts, "head", split_axis=2, concat_axis=0, tiled=True),
        lax.all_to_all(beta_parts, "head", split_axis=2, concat_axis=0, tiled=True),
    )
    k_blocks, w_rows, y_rows, trans_a, trans_b = block_factors(key_parts, value_parts, beta_parts)
    seq_rows = key_parts.shape[0]
    local_heads = key_parts.shape[2]
    blocks = seq_rows // CT
    block_steps = CT * REFL
    identity_heads = jnp.broadcast_to(
        jnp.eye(width_per_head, dtype=jnp.float32), (local_heads, width_per_head, width_per_head)
    )
    zero_heads = jnp.zeros((local_heads, width_per_head, width_per_head), jnp.float32)

    def compose(carried_pair, pieces):
        return (combine_pairs(carried_pair, pieces), None)

    device_pair, unused_rows = lax.scan(compose, (identity_heads, zero_heads), (trans_a, trans_b))
    device_a, device_b = device_pair

    def relay_step(counter, incoming):
        outgoing = matmul_heads(device_a, incoming) + device_b
        return shifted(outgoing, "seq", 1)

    start_state = lax.fori_loop(0, lax.axis_size("seq") - 1, relay_step, zero_heads)
    query_blocks = (
        unit_rows(query_parts[:, 0].astype(jnp.float32))
        .reshape(blocks, CT, local_heads, width_per_head)
        .transpose(0, 2, 1, 3)
    )
    step_iota = lax.broadcasted_iota(jnp.int32, (CT, block_steps), 1)
    token_iota = lax.broadcasted_iota(jnp.int32, (CT, block_steps), 0)
    causal = step_iota // REFL <= token_iota
    scores = jnp.where(
        causal,
        jnp.einsum("chtd,chid->chti", query_blocks, k_blocks, precision=highest),
        jnp.zeros((), jnp.float32),
    )

    def advance(carried, pieces):
        w_now, y_now, k_now, q_now, score_now = pieces
        update_rows = y_now - jnp.einsum("hid,hde->hie", w_now, carried, precision=highest)
        output = jnp.einsum("htd,hde->hte", q_now, carried, precision=highest) + jnp.einsum(
            "hti,hie->hte", score_now, update_rows, precision=highest
        )
        carried = carried + jnp.einsum("hid,hie->hde", k_now, update_rows, precision=highest)
        return (carried, output)

    final_state, outputs = lax.scan(
        advance, start_state, (w_rows, y_rows, k_blocks, query_blocks, scores)
    )
    outputs = outputs.transpose(0, 2, 1, 3).reshape(seq_rows, local_heads, width_per_head)
    normed = (
        outputs
        * lax.rsqrt(jnp.mean(outputs * outputs, axis=-1, keepdims=True) + epsilon)
        * norm_gain
    ).astype(jnp.bfloat16)
    normed = lax.all_to_all(normed, "head", split_axis=0, concat_axis=1, tiled=True)
    gated = normed.astype(jnp.float32).reshape(tok_rows, head_count * width_per_head) * jax.nn.silu(
        gate.astype(jnp.float32)
    )
    return gated.astype(jnp.bfloat16)


def solution(mesh):
    placed = (
        P(("seq", "head"), None),
        P(("seq", "head"), None, None),
        P(("seq", "head"), None, None),
        P(("seq", "head"), None, None),
        P(("seq", "head"), None),
        P(),
    )
    return jax.shard_map(
        shards, mesh=mesh, in_specs=placed, out_specs=P(("seq", "head"), None), check_vma=False
    )
```

profile of v0, /device:TPU:0, one launch (start us, length us, event | category | flops | bytes accessed | tf_op | source)
XLA Modules:
  0.0 767.5 jit_solution(11888366996750617239)
XLA Ops:
  30.9 6.2 copy.98
  37.1 6.2 copy.99
  51.1 5.5 all-to-all-done
  73.0 6.1 reshape.117
  79.2 10.2 %select_add_fusion = f32[4,4,256,256]{3,2,1,0:T(8,128)} fusion(f32[4,4,256,256]{3,2,1,0:T(8,128)} %reshape.117, f32[256,256]{1,0:T(8,128)S(1)} %copy-done.5, f32[4,4,256]{2,1,0:T(4,128)S(1)} %copy.96, pred[256,256]{1,0:T(8,128)(4,1)S(1)} %get-tuple-element.221), kind=kOutput, calls=%fused_computation.44 | convolution fusion | flops 3225419776 | bytes 8732672 | tf_op jit(solution)/shard_map/chid,chjd->chij/dot_general | solution.py:56
  89.5 9.5 %while.38 = (s32[]{:T(128)}, f32[4,4,256,256]{3,2,1,0:T(8,128)}, s32[2,2]{1,0:T(2,128)S(1)}, f32[2,4,4,128,128]{4,3,0,2,1:T(8,128)}, s32[]{:T(128)}) while((s32[]{:T(128)}, f32[4,4,256,256]{3,2,1,0:T(8,128)}, s32[2,2]{1,0:T(2,128)S(1)}, f32[2,4,4,128,128]{4,3,0,2,1:T(8,128)}, s32[]{:T(128)}) %tuple.71), condition=%wide.while_cond, body=%wide.while_body.sunk | while | flops 2 | bytes 2098785 | solution.py:58
  98.9 315.7 %custom-call.3 = f32[4,4,2,128,128]{3,4,2,1,0:T(8,128)S(1)} custom-call(f32[4,4,2,128,128]{4,3,2,1,0:T(8,128)} %bitcast.169), custom_call_target="InvertDiagBlocksLowerTriangular" | custom-call | tf_op jit(solution)/shard_map/triangular_solve | solution.py:58
  424.7 6.0 reshape.150
  435.4 5.8 fusion.30
  441.3 5.5 fusion.40
  454.2 8.5 %fusion.45 = f32[4,4,256,256]{3,2,1,0:T(8,128)} fusion(f32[4,4,256,256]{3,2,1,0:T(8,128)S(1)} %copy-done, f32[4,4,256,256]{3,2,1,0:T(8,128)S(1)} %get-tuple-element.414), kind=kOutput, calls=%fused_computation.89 | convolution fusion | flops 3221225472 | bytes 12582912 | tf_op jit(solution)/shard_map/chid,chie->chde/dot_general | solution.py:69
  462.7 8.7 %convolution_subtract_fusion.1 = f32[4,4,256,256]{3,2,1,0:T(8,128)} fusion(f32[4,4,256,256]{3,2,1,0:T(8,128)S(1)} %copy-done, f32[4,4,256,256]{3,2,1,0:T(8,128)S(1)} %get-tuple-element.415, f32[256,256]{1,0:T(8,128)S(1)} %fusion.42), kind=kOutput, calls=%fused_computation.48 | convolution fusion | flops 3222274048 | bytes 12845056 | tf_op jit(solution)/shard_map/chid,chie->chde/dot_general | solution.py:68
  471.5 21.1 %while.39 = (s32[]{:T(128)}, f32[4,256,256]{2,1,0:T(8,128)S(1)}, f32[4,256,256]{2,1,0:T(8,128)S(1)}, f32[4,4,256,256]{3,2,1,0:T(8,128)}, f32[4,4,256,256]{3,2,1,0:T(8,128)}, /*index=5*/s32[]{:T(128)}, s32[]{:T(128)}) while((s32[]{:T(128)}, f32[4,256,256]{2,1,0:T(8,128)S(1)}, f32[4,256,256]{2,1,0:T(8,128)S(1)}, ...), condition=%wide.region_2.3_spmd.clone, body=%wide.region_1.2_spmd.clone.sunk | while | flops 1611137024 | bytes 11535959 | solution.py:100
  492.6 8.4 %convolution_select_fusion = f32[4,4,128,256]{3,2,1,0:T(8,128)} fusion(f32[4,4,128,256]{3,2,1,0:T(8,128)} %divide_bitcast_fusion, f32[4,4,256,256]{3,2,1,0:T(8,128)} %reshape.117, pred[128,256]{1,0:T(8,128)(4,1)S(1)} %iota_compare_fusion.3), kind=kOutput, calls=%fused_computation.63 | convolution fusion | flops 1611137024 | bytes 8421376 | tf_op jit(solution)/shard_map/chtd,chid->chti/dot_general | solution.py:118
  501.1 193.5 %while.36 = (s32[]{:T(128)}, f32[4,256,256]{2,1,0:T(8,128)S(1)}, f32[4,256,256]{2,1,0:T(8,128)S(1)}, f32[4,256,256]{2,1,0:T(8,128)S(1)}, s32[]{:T(128)}) while((s32[]{:T(128)}, f32[4,256,256]{2,1,0:T(8,128)S(1)}, f32[4,256,256]{2,1,0:T(8,128)S(1)}, f32[4,256,256]{2,1,0:T(8,128)S(1)}, s32[]{:T(128)}) %tuple.77), condition=%wide.region_4.5_spmd, body=%wide.region_3.4_spmd.sunk | while | flops 805568512 | bytes 8388709 | solution.py:107
  507.2 23.3 %collective-permute-done = f32[4,256,256]{2,1,0:T(8,128)S(1)} collective-permute-done((f32[4,256,256]{2,1,0:T(8,128)}, f32[4,256,256]{2,1,0:T(8,128)S(1)}, u32[]{:S(2)}, u32[]{:S(2)}) %collective-permute-start) | collective-permute-done | bytes 1048608 | tf_op jit(solution)/shard_map/while/body/eval_jaxpr/ppermute | solution.py:17
  537.0 22.4 %collective-permute-done = f32[4,256,256]{2,1,0:T(8,128)S(1)} collective-permute-done((f32[4,256,256]{2,1,0:T(8,128)}, f32[4,256,256]{2,1,0:T(8,128)S(1)}, u32[]{:S(2)}, u32[]{:S(2)}) %collective-permute-start) | collective-permute-done | bytes 1048608 | tf_op jit(solution)/shard_map/while/body/eval_jaxpr/ppermute | solution.py:17
  565.9 21.6 %collective-permute-done = f32[4,256,256]{2,1,0:T(8,128)S(1)} collective-permute-done((f32[4,256,256]{2,1,0:T(8,128)}, f32[4,256,256]{2,1,0:T(8,128)S(1)}, u32[]{:S(2)}, u32[]{:S(2)}) %collective-permute-start) | collective-permute-done | bytes 1048608 | tf_op jit(solution)/shard_map/while/body/eval_jaxpr/ppermute | solution.py:17
  594.8 20.7 %collective-permute-done = f32[4,256,256]{2,1,0:T(8,128)S(1)} collective-permute-done((f32[4,256,256]{2,1,0:T(8,128)}, f32[4,256,256]{2,1,0:T(8,128)S(1)}, u32[]{:S(2)}, u32[]{:S(2)}) %collective-permute-start) | collective-permute-done | bytes 1048608 | tf_op jit(solution)/shard_map/while/body/eval_jaxpr/ppermute | solution.py:17
  622.9 19.9 %collective-permute-done = f32[4,256,256]{2,1,0:T(8,128)S(1)} collective-permute-done((f32[4,256,256]{2,1,0:T(8,128)}, f32[4,256,256]{2,1,0:T(8,128)S(1)}, u32[]{:S(2)}, u32[]{:S(2)}) %collective-permute-start) | collective-permute-done | bytes 1048608 | tf_op jit(solution)/shard_map/while/body/eval_jaxpr/ppermute | solution.py:17
  650.1 19.0 %collective-permute-done = f32[4,256,256]{2,1,0:T(8,128)S(1)} collective-permute-done((f32[4,256,256]{2,1,0:T(8,128)}, f32[4,256,256]{2,1,0:T(8,128)S(1)}, u32[]{:S(2)}, u32[]{:S(2)}) %collective-permute-start) | collective-permute-done | bytes 1048608 | tf_op jit(solution)/shard_map/while/body/eval_jaxpr/ppermute | solution.py:17
  676.5 18.2 %collective-permute-done = f32[4,256,256]{2,1,0:T(8,128)S(1)} collective-permute-done((f32[4,256,256]{2,1,0:T(8,128)}, f32[4,256,256]{2,1,0:T(8,128)S(1)}, u32[]{:S(2)}, u32[]{:S(2)}) %collective-permute-start) | collective-permute-done | bytes 1048608 | tf_op jit(solution)/shard_map/while/body/eval_jaxpr/ppermute | solution.py:17
  694.7 42.1 %while.37 = (s32[]{:T(128)}, f32[4,256,256]{2,1,0:T(8,128)S(1)}, f32[4,4,128,256]{3,2,0,1:T(8,128)}, f32[4,4,256,256]{3,2,1,0:T(8,128)}, f32[4,4,256,256]{3,2,1,...) while((s32[]{:T(128)}, f32[4,256,256]{2,1,0:T(8,128)S(1)}, ...), condition=%wide.region_7.8_spmd, body=%wide.region_6.7_spmd.sunk | while | flops 2416574464 | bytes 13110365 | solution.py:131
  747.4 13.1 %all-to-all-done.4 = bf16[512,4,256]{2,1,0:T(4,128)(2,1)S(1)} async-done(((bf16[512,4,256]{2,1,0:T(4,128)(2,1)}), bf16[512,4,256]{2,1,0:T(4,128)(2,1)S(1)}, u32[]{:S(2)}, u32[]{:S(2)}) %all-to-all-start.4) | async-done | bytes 1048608 | tf_op jit(solution)/shard_map/all_to_all | solution.py:140
  (129 shorter events, 215.2 us)
Async XLA Ops:
  1.3 8.1 %all-to-all-start.1 = ((bf16[128,2,16,1]{0,1,3,2:T(2,128)(2,1)}), bf16[128,2,16,1]{0,1,3,2:T(2,128)(2,1)S(1)}, u32[]{:S(2)}, u32[]{:S(2)}) async-start(bf16[128,2,16,1]{0,1,3,2:T(2,128)(2,1)} %bitcast.117), calls=%async_computation.1 | async-start | bytes 16384 | tf_op jit(solution)/shard_map/all_to_all | solution.py:85
  9.4 17.9 %all-to-all-start.3 = ((bf16[128,1,16,256]{3,0,1,2:T(8,128)(2,1)}), bf16[128,1,16,256]{3,0,1,2:T(8,128)(2,1)S(1)}, u32[]{:S(2)}, u32[]{:S(2)}) async-start(bf16[128,1,16,256]{3,0,1,2:T(8,128)(2,1)} %copy.106), calls=%async_computation.3 | async-start | bytes 2097152 | tf_op jit(solution)/shard_map/all_to_all | solution.py:82
  27.3 3.6 copy-start.3
  27.3 29.2 %all-to-all-start = ((bf16[128,2,16,256]{3,1,0,2:T(2,128)(2,1)}), bf16[128,2,16,256]{3,1,0,2:T(2,128)(2,1)S(1)}, u32[]{:S(2)}, u32[]{:S(2)}) async-start(bf16[128,2,16,256]{3,1,0,2:T(2,128)(2,1)} %copy.90), calls=%async_computation | async-start | bytes 4194304 | tf_op jit(solution)/shard_map/all_to_all | solution.py:83
  56.5 362.8 %all-to-all-start.2 = ((bf16[128,2,16,256]{3,1,0,2:T(2,128)(2,1)}), bf16[128,2,16,256]{3,1,0,2:T(2,128)(2,1)}, u32[]{:S(2)}, u32[]{:S(2)}) async-start(bf16[128,2,16,256]{3,1,0,2:T(2,128)(2,1)} %copy.99), calls=%async_computation.2 | async-start | bytes 4194304 | tf_op jit(solution)/shard_map/all_to_all | solution.py:84
  67.5 1.8 copy-start.4
  73.0 6.1 copy-start.5
  79.2 10.2 %copy-start.8 = (s32[2]{0:T(128)S(1)}, s32[2]{0:T(128)}, u32[]{:S(2)}) copy-start(s32[2]{0:T(128)} %iota_multiply_fusion) | copy-start | bytes 28
  435.4 11.4 %slice-start = ((s8[8388608]{0:T(1024)(128)(4,1)}), s8[4194304]{0:T(1024)(128)(4,1)S(1)}, s32[]{:S(2)}) async-start(s8[8388608]{0:T(1024)(128)(4,1)} %bitcast.156), calls=%async_computation.5 | async-start | bytes 8388608
  441.2 5.6 slice-start.1
  450.9 3.3 copy-start
  451.7 11.0 %copy-start.1 = (f32[4,4,256,256]{3,2,1,0:T(8,128)}, f32[4,4,256,256]{3,2,1,0:T(8,128)S(1)}, u32[]{:S(2)}) copy-start(f32[4,4,256,256]{3,2,1,0:T(8,128)S(1)} %get-tuple-element.414) | copy-start | bytes 12582916
  451.7 11.0 %copy-start.2 = (f32[4,4,256,256]{3,2,1,0:T(8,128)}, f32[4,4,256,256]{3,2,1,0:T(8,128)S(1)}, u32[]{:S(2)}) copy-start(f32[4,4,256,256]{3,2,1,0:T(8,128)S(1)} %get-tuple-element.415) | copy-start | bytes 12582916
  503.3 27.2 %collective-permute-start = (f32[4,256,256]{2,1,0:T(8,128)}, f32[4,256,256]{2,1,0:T(8,128)S(1)}, u32[]{:S(2)}, u32[]{:S(2)}) collective-permute-start(f32[4,256,256]{2,1,0:T(8,128)} %convolution_add_fusion.7), channel_id=1, source_target_pairs={{0,4},{4,8},{8,12},{12,16},{16,20},{20,24},{24,28},{1,5},{5,9},{9,... | collective-permute-start | bytes 3145736 | tf_op jit(solution)/shard_map/while/body/eval_jaxpr/ppermute | solution.py:17
  532.6 26.8 %collective-permute-start = (f32[4,256,256]{2,1,0:T(8,128)}, f32[4,256,256]{2,1,0:T(8,128)S(1)}, u32[]{:S(2)}, u32[]{:S(2)}) collective-permute-start(f32[4,256,256]{2,1,0:T(8,128)} %convolution_add_fusion.7), channel_id=1, source_target_pairs={{0,4},{4,8},{8,12},{12,16},{16,20},{20,24},{24,28},{1,5},{5,9},{9,... | collective-permute-start | bytes 3145736 | tf_op jit(solution)/shard_map/while/body/eval_jaxpr/ppermute | solution.py:17
  561.5 26.0 %collective-permute-start = (f32[4,256,256]{2,1,0:T(8,128)}, f32[4,256,256]{2,1,0:T(8,128)S(1)}, u32[]{:S(2)}, u32[]{:S(2)}) collective-permute-start(f32[4,256,256]{2,1,0:T(8,128)} %convolution_add_fusion.7), channel_id=1, source_target_pairs={{0,4},{4,8},{8,12},{12,16},{16,20},{20,24},{24,28},{1,5},{5,9},{9,... | collective-permute-start | bytes 3145736 | tf_op jit(solution)/shard_map/while/body/eval_jaxpr/ppermute | solution.py:17
  589.6 26.0 %collective-permute-start = (f32[4,256,256]{2,1,0:T(8,128)}, f32[4,256,256]{2,1,0:T(8,128)S(1)}, u32[]{:S(2)}, u32[]{:S(2)}) collective-permute-start(f32[4,256,256]{2,1,0:T(8,128)} %convolution_add_fusion.7), channel_id=1, source_target_pairs={{0,4},{4,8},{8,12},{12,16},{16,20},{20,24},{24,28},{1,5},{5,9},{9,... | collective-permute-start | bytes 3145736 | tf_op jit(solution)/shard_map/while/body/eval_jaxpr/ppermute | solution.py:17
  617.7 25.1 %collective-permute-start = (f32[4,256,256]{2,1,0:T(8,128)}, f32[4,256,256]{2,1,0:T(8,128)S(1)}, u32[]{:S(2)}, u32[]{:S(2)}) collective-permute-start(f32[4,256,256]{2,1,0:T(8,128)} %convolution_add_fusion.7), channel_id=1, source_target_pairs={{0,4},{4,8},{8,12},{12,16},{16,20},{20,24},{24,28},{1,5},{5,9},{9,... | collective-permute-start | bytes 3145736 | tf_op jit(solution)/shard_map/while/body/eval_jaxpr/ppermute | solution.py:17
  644.9 24.3 %collective-permute-start = (f32[4,256,256]{2,1,0:T(8,128)}, f32[4,256,256]{2,1,0:T(8,128)S(1)}, u32[]{:S(2)}, u32[]{:S(2)}) collective-permute-start(f32[4,256,256]{2,1,0:T(8,128)} %convolution_add_fusion.7), channel_id=1, source_target_pairs={{0,4},{4,8},{8,12},{12,16},{16,20},{20,24},{24,28},{1,5},{5,9},{9,... | collective-permute-start | bytes 3145736 | tf_op jit(solution)/shard_map/while/body/eval_jaxpr/ppermute | solution.py:17
  671.3 23.4 %collective-permute-start = (f32[4,256,256]{2,1,0:T(8,128)}, f32[4,256,256]{2,1,0:T(8,128)S(1)}, u32[]{:S(2)}, u32[]{:S(2)}) collective-permute-start(f32[4,256,256]{2,1,0:T(8,128)} %convolution_add_fusion.7), channel_id=1, source_target_pairs={{0,4},{4,8},{8,12},{12,16},{16,20},{20,24},{24,28},{1,5},{5,9},{9,... | collective-permute-start | bytes 3145736 | tf_op jit(solution)/shard_map/while/body/eval_jaxpr/ppermute | solution.py:17
  694.7 44.1 %copy-start.7 = (f32[256]{0:T(256)S(1)}, f32[256]{0:T(256)}, u32[]{:S(2)}) copy-start(f32[256]{0:T(256)} %param.17) | copy-start | bytes 3076
  738.7 7.4 copy-start.6
  742.6 17.9 %all-to-all-start.4 = ((bf16[512,4,256]{2,1,0:T(4,128)(2,1)}), bf16[512,4,256]{2,1,0:T(4,128)(2,1)S(1)}, u32[]{:S(2)}, u32[]{:S(2)}) async-start(bf16[512,4,256]{2,1,0:T(4,128)(2,1)} %copy.109), calls=%async_computation.4 | async-start | bytes 2097152 | tf_op jit(solution)/shard_map/all_to_all | solution.py:140
where the time goes:
time: 775 us; the launch traced here: 768 us
  other arithmetic  344 us (44%)
  waiting for transfers between devices  170 us (22%)
  matrix products  128 us (17%)
  local copies, waits for them, and re-layouts  71.1 us (9%)
  starting transfers between devices  53.2 us (7%)
    another operation x4, other arithmetic, block_factors(): lax.linalg.triangular_solve(lower_part, jnp.concatenate([k_blocks, v_bloc...  317 us
    ppermute x7, waiting for transfers between devices, shifted(): return lax.ppermute(block, axis, route)  145 us
    dot_general x15, matrix products, matmul_heads(): return jnp.einsum('hde,hef->hdf', left_side, right_side, precision=highest)  35.1 us
    ppermute x7, starting transfers between devices, shifted(): return lax.ppermute(block, axis, route)  33.6 us
    unnamed x29, local copies, waits for them, and re-layouts  22.5 us
  transfers between devices with their start and end apart: 12, of which 11 were waited for; matrix products, arithmetic and copies ran while one was open for 51% of the time, Pallas kernels for 0%

commit v1 on v0

v1 whole, which is shorter than its diff:
```python
import functools

import jax
import jax.numpy as jnp
from jax import lax
from jax.experimental import pallas as pl
from jax.experimental.pallas import tpu as pltpu
from jax.sharding import Mesh, PartitionSpec as P

EPS = 1e-06
F32 = jnp.float32
BF16 = jnp.bfloat16
PAD = 16
PER_STEP = 2

NN = ((1,), (0,))
NT = ((1,), (1,))
TN = ((0,), (0,))


def dot(a, b, dims=NN):
    return lax.dot_general(a, b, (dims, ((), ())), preferred_element_type=F32)


def split(x):
    hi = x.astype(BF16)
    return hi, (x - hi.astype(F32)).astype(BF16)


def dot3(a, b, dims=NN):
    return dot(a[0], b[0], dims) + (dot(a[0], b[1], dims) + dot(a[1], b[0], dims))


def dot2r(a, b, dims=NN):
    return dot(a, b[0], dims) + dot(a, b[1], dims)


def dot2l(a, b, dims=NN):
    return dot(a[0], b, dims) + dot(a[1], b, dims)


def put(ref, i, parts):
    ref[i, 0] = parts[0]
    ref[i, 1] = parts[1]


def get(ref, i):
    return ref[i, 0], ref[i, 1]


def inverse(grams, g_rows):
    n = grams[0].shape[0]
    row = lax.broadcasted_iota(jnp.int32, (n, n), 0)
    col = lax.broadcasted_iota(jnp.int32, (n, n), 1)
    eye = row == col
    pair = (row // 2 == col // 2) & (row > col)
    out = []
    for gram, g_row in zip(grams, g_rows):
        diag = jnp.where(eye, g_row, 0.0)
        g_col = jnp.sum(diag, axis=1, keepdims=True)
        out.append(diag - jnp.where(pair, g_col * (gram * g_row), 0.0))
    parts = [split(gram) for gram in grams]
    size = 2
    while size < n:
        if size < 8:
            mask = (row // (2 * size) == col // (2 * size)) & (row // size > col // size)
            sp = [split(t) for t in out]
            mid = [split(jnp.where(mask, dot3(t, p), 0.0)) for t, p in zip(sp, parts)]
            out = [t - dot3(m, s) for t, m, s in zip(out, mid, sp)]
        else:
            half = n // 2
            r = lax.broadcasted_iota(jnp.int32, (half, n), 0)
            c = lax.broadcasted_iota(jnp.int32, (half, n), 1)
            mask = c // size == 2 * (r // size)
            cuts = range(0, n, 2 * size)
            odd = [jnp.concatenate([t[i + size : i + 2 * size] for i in cuts], axis=0) for t in out]
            sp = [split(t) for t in out]
            mid = [
                split(jnp.where(mask, dot3(split(o), p), 0.0)) for o, p in zip(odd, parts)
            ]
            low = [o - dot3(m, s) for o, m, s in zip(odd, mid, sp)]
            out = [
                jnp.concatenate(
                    [
                        piece
                        for j, i in enumerate(cuts)
                        for piece in (t[i : i + size], l[j * size : (j + 1) * size])
                    ],
                    axis=0,
                )
                for t, l in zip(out, low)
            ]
        size *= 2
    return out


def keys_kernel(k_ref, ty_ref, w_ref, r_ref, xa_ref, fin_ref, state):
    per, steps, width = k_ref.shape
    steps -= PAD

    @pl.when(pl.program_id(0) == 0)
    def _():
        a = lax.broadcasted_iota(jnp.int32, (width, width), 0)
        b = lax.broadcasted_iota(jnp.int32, (width, width), 1)
        state[...] = jnp.where(a == b, 1.0, 0.0)

    row = lax.broadcasted_iota(jnp.int32, (steps, steps), 0)
    col = lax.broadcasted_iota(jnp.int32, (steps, steps), 1)
    ks = [k_ref[i, :steps] for i in range(per)]
    grams = [dot(k, k, NT) for k in ks]
    sq = [jnp.sum(jnp.where(row == col, g, 0.0), axis=0, keepdims=True) + EPS for g in grams]
    g_rows = [
        k_ref[i, steps : steps + PAD].astype(F32)[0:1] / s for i, s in enumerate(sq)
    ]
    inv = inverse(grams, g_rows)
    for i in range(per):
        put(ty_ref, i, split(inv[i] * jnp.sqrt(sq[i])))
    ws = [split(dot2l(split(t), k)) for t, k in zip(inv, ks)]
    rs = [split(dot2r(k, w, TN)) for k, w in zip(ks, ws)]
    x = state[...]
    for i in range(per):
        put(w_ref, i, ws[i])
        put(r_ref, i, rs[i])
        parts = split(x)
        put(xa_ref, i, parts)
        x = x - dot3(rs[i], parts)
    state[...] = x
    fin_ref[...] = x


def values_kernel(k_ref, v_ref, ty_ref, r_ref, y_ref, xb_ref, fin_ref, state):
    per, steps, width = v_ref.shape

    @pl.when(pl.program_id(0) == 0)
    def _():
        state[...] = jnp.zeros_like(state)

    ys = [split(dot2l(get(ty_ref, i), v_ref[i])) for i in range(per)]
    bs = [dot2r(k_ref[i, :steps], ys[i], TN) for i in range(per)]
    x = state[...]
    for i in range(per):
        put(y_ref, i, ys[i])
        parts = split(x)
        put(xb_ref, i, parts)
        x = x + (bs[i] - dot3(get(r_ref, i), parts))
    state[...] = x
    fin_ref[...] = x


def queries_kernel(q_ref, k_ref, w_ref, y_ref, xa_ref, xb_ref, o_ref, qt_ref):
    per, toks, width = q_ref.shape
    steps = w_ref.shape[2]
    refl = steps // toks
    tok = lax.broadcasted_iota(jnp.int32, (toks, steps), 0)
    step = lax.broadcasted_iota(jnp.int32, (toks, steps), 1)
    causal = step // refl <= tok
    for i in range(per):
        q = q_ref[i]
        qf = q.astype(F32)
        inv = 1.0 / jnp.sqrt(jnp.sum(qf * qf, axis=1, keepdims=True) + EPS)
        s = split(jnp.where(causal, dot(q, k_ref[i, :steps], NT), 0.0))
        qw = split(qf - dot3(s, get(w_ref, i)))
        o_ref[i] = inv * (dot3(qw, get(xb_ref, i)) + dot3(s, get(y_ref, i)))
        qt_ref[i] = inv * dot3(qw, get(xa_ref, i))


def finish_kernel(o_ref, qt_ref, s_ref, gain_ref, out_ref):
    per = o_ref.shape[0]
    s = split(s_ref[...])
    for i in range(per):
        o = o_ref[i] + dot3(split(qt_ref[i]), s)
        mean = jnp.mean(o * o, axis=1, keepdims=True)
        out_ref[i] = (o * lax.rsqrt(mean + EPS) * gain_ref[...]).astype(BF16)


def gate_kernel(n_ref, gate_ref, out_ref):
    per, toks, width = n_ref.shape
    for i in range(per):
        g = gate_ref[:, i * width : (i + 1) * width].astype(F32)
        out_ref[:, i * width : (i + 1) * width] = (
            n_ref[i].astype(F32) * (g / (1.0 + jnp.exp(-g)))
        ).astype(BF16)


def call(kernel, grid, ins, outs, scratch=(), name=None):
    def spec(a, per):
        if per is None:
            return pl.BlockSpec(a.shape, lambda c: (0,) * len(a.shape))
        return pl.BlockSpec((per,) + a.shape[1:], lambda c: (c,) + (0,) * (len(a.shape) - 1))

    return pl.pallas_call(
        kernel,
        grid=(grid,),
        in_specs=[spec(*i) for i in ins],
        out_specs=[spec(*o) for o in outs],
        out_shape=[o[0] for o in outs],
        scratch_shapes=list(scratch),
        name=name,
        compiler_params=pltpu.CompilerParams(dimension_semantics=("arbitrary",)),
    )(*[i[0] for i in ins])


def shards(queries, keys, values, betas, gate, norm_gain):
    toks = queries.shape[0]
    refl = keys.shape[1]
    width = norm_gain.shape[0]
    heads = queries.shape[1] // width
    steps = toks * refl
    near = ("near", "head")
    far_size = lax.axis_size("far")
    group = lax.axis_size("near") * lax.axis_size("head")
    own = heads // group

    def by_head(x, rows):
        return x.reshape(rows, heads, width).transpose(1, 0, 2)

    def exchange(x):
        return lax.all_to_all(x, near, 0, 0, tiled=True)

    b_rows = jnp.broadcast_to(betas.reshape(steps, heads).T[:, None, :], (heads, PAD, steps))
    k = exchange(jnp.concatenate([by_head(keys, steps), b_rows], axis=1))
    v = exchange(by_head(values, steps))
    q = exchange(by_head(queries, toks))

    blocks = group
    per = PER_STEP
    grid = blocks // per
    sds = jax.ShapeDtypeStruct
    pair = sds((blocks, 2, width, width), BF16)
    rows = sds((blocks, 2, steps, width), BF16)
    state = sds((width, width), F32)
    scratch = (pltpu.VMEM((width, width), F32),)
    ty, w, r, xa, end_a = call(
        keys_kernel,
        grid,
        [(k, per)],
        [
            (sds((blocks, 2, steps, steps), BF16), per),
            (rows, per),
            (pair, per),
            (pair, per),
            (state, None),
        ],
        scratch,
        "keys",
    )
    y, xb, end_b = call(
        values_kernel,
        grid,
        [(k, per), (v, per), (ty, per), (r, per)],
        [(rows, per), (pair, per), (state, None)],
        scratch,
        "values",
    )
    route = [(i, i + 1) for i in range(far_size - 1)]
    start = lax.ppermute(end_b, "far", route)
    for _ in range(far_size - 2):
        sent = jnp.dot(end_a, start, precision=lax.Precision.HIGHEST) + end_b
        start = lax.ppermute(sent, "far", route)
    toks_out = sds((blocks, toks, width), F32)
    o, qt = call(
        queries_kernel,
        grid,
        [(q, per), (k, per), (w, per), (y, per), (xa, per), (xb, per)],
        [(toks_out, per), (toks_out, per)],
        (),
        "queries",
    )
    (normed,) = call(
        finish_kernel,
        grid,
        [(o, per), (qt, per), (start, None), (norm_gain[None, :], None)],
        [(sds((blocks, toks, width), BF16), per)],
        (),
        "finish",
    )
    normed = exchange(normed)
    wide = 4
    return pl.pallas_call(
        gate_kernel,
        grid=(heads // wide,),
        in_specs=[
            pl.BlockSpec((wide, toks, width), lambda c: (c, 0, 0)),
            pl.BlockSpec((toks, wide * width), lambda c: (0, c)),
        ],
        out_specs=pl.BlockSpec((toks, wide * width), lambda c: (0, c)),
        out_shape=sds((toks, heads * width), BF16),
        name="gate",
        compiler_params=pltpu.CompilerParams(dimension_semantics=("arbitrary",)),
    )(normed, gate)


def solution(mesh):
    def step(queries, keys, values, betas, gate, norm_gain):
        heads = queries.shape[1] // norm_gain.shape[0]
        seq, head = mesh.shape["seq"], mesh.shape["head"]
        near = heads // head
        fine = Mesh(mesh.devices.reshape(seq // near, near, head), ("far", "near", "head"))
        lead = ("far", "near", "head")
        placed = (
            P(lead, None),
            P(lead, None, None),
            P(lead, None, None),
            P(lead, None, None),
            P(lead, None),
            P(),
        )
        return jax.shard_map(
            shards, mesh=fine, in_specs=placed, out_specs=P(lead, None), check_vma=False
        )(queries, keys, values, betas, gate, norm_gain)

    return step
```

time: 775 us -> 187 us (0.24)
  other arithmetic: 344 us -> 3.11 us
  matrix products: 128 us -> 0 us
  waiting for transfers between devices: 170 us -> 45.4 us
  Pallas kernels: 0 us -> 75 us
  local copies, waits for them, and re-layouts: 71.1 us -> 19.3 us
  starting transfers between devices: 53.2 us -> 21.4 us
  blocking collectives: 0 us -> 21.3 us
    another operation x4 -> x0, other arithmetic: 317 us -> none  [block_factors(): lax.linalg.triangular_solve(lower_part, jnp.concatenate([k_blocks, v_bloc...]
    ppermute x7 -> x1, waiting for transfers between devices: 145 us -> 0.01 us  [shards(): start = lax.ppermute(end_b, 'far', route)]
    dot_general x35 -> x0, matrix products: 113 us -> none  [the longest x15 35.1 us: matmul_heads(): return jnp.einsum('hde,hef->hdf', left_side, right_side, precision=highest)]
    pallas_call x0 -> x5, Pallas kernels: none -> 75 us  [the longest x4 71.1 us: call(): pl.pallas_call(kernel, grid=(grid,), in_specs=[spec(*i) for i in ins], ou...]
    ppermute x7 -> x1, starting transfers between devices: 33.6 us -> 4.5 us  [shards(): start = lax.ppermute(end_b, 'far', route)]
    all_to_all x0 -> x1, blocking collectives: none -> 21.3 us  [exchange(): return lax.all_to_all(x, near, 0, 0, tiled=True)]
    all_to_all x5 -> x3, waiting for transfers between devices: 24.6 us -> 45.4 us  [exchange(): return lax.all_to_all(x, near, 0, 0, tiled=True)]
    unnamed x29 -> x12, local copies, waits for them, and re-layouts: 22.5 us -> 4.74 us
  transfers between devices with their start and end apart: 12 -> 4, of which waited for: 11 -> 2; matrix products, arithmetic and copies ran while one was open for 51% -> 8% of each run, Pallas kernels for 0% -> 34%
where the time goes in v1:
time: 187 us; the launch traced here: 186 us
  Pallas kernels  75 us (40%)
  waiting for transfers between devices  45.4 us (24%)
  starting transfers between devices  21.4 us (11%)
  blocking collectives  21.3 us (11%)
  local copies, waits for them, and re-layouts  19.3 us (10%)
  other arithmetic  3.11 us (2%)
    pallas_call x4, Pallas kernels, call(): pl.pallas_call(kernel, grid=(grid,), in_specs=[spec(*i) for i in ins], ou...  71.1 us
    all_to_all x3, waiting for transfers between devices, exchange(): return lax.all_to_all(x, near, 0, 0, tiled=True)  45.4 us
    all_to_all x1, blocking collectives, exchange(): return lax.all_to_all(x, near, 0, 0, tiled=True)  21.3 us
    all_to_all x3, starting transfers between devices, exchange(): return lax.all_to_all(x, near, 0, 0, tiled=True)  16.9 us
    reshape x5, local copies, waits for them, and re-layouts, by_head(): return x.reshape(rows, heads, width).transpose(1, 0, 2)  14.5 us
    unnamed x12, local copies, waits for them, and re-layouts  4.74 us
    ppermute x1, starting transfers between devices, shards(): start = lax.ppermute(end_b, 'far', route)  4.5 us
    pallas_call x1, Pallas kernels, shards(): pl.pallas_call(gate_kernel, grid=(heads // wide,), in_specs=[pl.BlockSpec...  3.85 us
  transfers between devices with their start and end apart: 4, of which 2 were waited for; matrix products, arithmetic and copies ran while one was open for 8% of the time, Pallas kernels for 34%

profile of v1, /device:TPU:0, one launch (start us, length us, event | category | flops | bytes accessed | tf_op | source)
XLA Modules:
  0.0 185.8 jit_solution(484582520450563523)
XLA Ops:
  0.0 3.1 %reshape.16 = bf16[256,16,256]{2,1,0:T(8,128)(2,1)S(1)} reshape(bf16[128,2,4096]{2,1,0:T(2,128)(2,1)} %param.8) | data formatting | bytes 4194304 | tf_op jit(solution)/shard_map/reshape | solution.py:215
  3.2 2.0 %copy.15 = bf16[256,16,256]{2,0,1:T(8,128)(2,1)} copy(bf16[256,16,256]{2,1,0:T(8,128)(2,1)S(1)} %reshape.16) | data formatting | bytes 4194304 | tf_op jit(solution)/shard_map/reshape | solution.py:215
  5.2 6.3 %all-to-all-start.2 = ((bf16[16,256,256]{2,1,0:T(8,128)(2,1)}), bf16[16,256,256]{2,1,0:T(8,128)(2,1)S(1)}, u32[]{:S(2)}, u32[]{:S(2)}) async-start(bf16[16,256,256]{2,1,0:T(8,128)(2,1)} %bitcast.12), calls=%async_computation.2 | async-start | bytes 4194304 | tf_op jit(solution)/shard_map/all_to_all | solution.py:218
  11.5 4.4 %reshape.14 = bf16[256,16,256]{2,1,0:T(8,128)(2,1)} reshape(bf16[128,2,4096]{2,1,0:T(2,128)(2,1)} %param.7) | data formatting | bytes 4194304 | tf_op jit(solution)/shard_map/reshape | solution.py:215
  15.9 3.7 %copy.16 = bf16[256,16,256]{2,0,1:T(8,128)(2,1)} copy(bf16[256,16,256]{2,1,0:T(8,128)(2,1)} %reshape.14) | data formatting | bytes 4194304 | tf_op jit(solution)/shard_map/reshape | solution.py:215
  19.5 0.1 copy.10
  19.7 0.1 copy.11
  19.8 3.1 %pad_maximum_fusion = bf16[16,272,256]{2,1,0:T(8,128)(2,1)} fusion(bf16[16,16,256]{2,1,0:T(8,128)(2,1)S(1)} %broadcast_in_dim.4, bf16[16,256,256]{2,1,0:T(8,128)(2,1)} %bitcast.13), kind=kLoop, calls=%fused_computation | loop fusion | flops 4456448 | bytes 4456448 | tf_op jit(solution)/shard_map/concatenate | solution.py:221
  22.9 17.7 %all-to-all-done.2.v_ref = bf16[16,256,256]{2,1,0:T(8,128)(2,1)S(1)} async-done(((bf16[16,256,256]{2,1,0:T(8,128)(2,1)}), bf16[16,256,256]{2,1,0:T(8,128)(2,1)S(1)}, u32[]{:S(2)}, u32[]{:S(2)}) %all-to-all-start.2) | async-done | bytes 2097184 | tf_op jit(solution)/shard_map/all_to_all | solution.py:218
  40.6 1.3 copy-done.1
  41.9 4.9 %all-to-all-start.1 = ((bf16[16,272,256]{2,1,0:T(8,128)(2,1)}), bf16[16,272,256]{2,1,0:T(8,128)(2,1)S(1)}, u32[]{:S(2)}, u32[]{:S(2)}) async-start(bf16[16,272,256]{2,1,0:T(8,128)(2,1)} %pad_maximum_fusion), calls=%async_computation.1 | async-start | bytes 4456448 | tf_op jit(solution)/shard_map/all_to_all | solution.py:218
  46.8 1.6 copy.7
  48.4 1.3 copy.8
  49.7 27.7 %all-to-all-done.1.k_ref = bf16[16,272,256]{2,1,0:T(8,128)(2,1)S(1)} async-done(((bf16[16,272,256]{2,1,0:T(8,128)(2,1)}), bf16[16,272,256]{2,1,0:T(8,128)(2,1)S(1)}, u32[]{:S(2)}, u32[]{:S(2)}) %all-to-all-start.1) | async-done | bytes 2228256 | tf_op jit(solution)/shard_map/all_to_all | solution.py:218
  77.5 5.7 %all-to-all-start = ((bf16[16,128,256]{2,1,0:T(8,128)(2,1)}), bf16[16,128,256]{2,1,0:T(8,128)(2,1)S(1)}, u32[]{:S(2)}, u32[]{:S(2)}) async-start(bf16[16,128,256]{2,1,0:T(8,128)(2,1)} %bitcast.14), calls=%async_computation | async-start | bytes 2097152 | tf_op jit(solution)/shard_map/all_to_all | solution.py:218
  83.2 38.0 %keys.1 = (bf16[16,2,256,256]{3,2,1,0:T(8,128)(2,1)}, bf16[16,2,256,256]{3,2,1,0:T(8,128)(2,1)}, bf16[16,2,256,256]{3,2,1,0:T(8,128)(2,1)}, bf16[16,2,256,256]{3,2,1,0:T(8,128)(2,1)}, f32[256,256]{1,0:T(8,128)}) custom-call(bf16[16,272,256]{2,1,0:T(8,128)(2,1)} %copy-done), custom_call_target="tpu_custom_call" | custom-call | tf_op jit(solution)/shard_map/keys/pallas_call | solution.py:191
  121.2 11.9 %values.1 = (bf16[16,2,256,256]{3,2,1,0:T(8,128)(2,1)}, bf16[16,2,256,256]{3,2,1,0:T(8,128)(2,1)}, f32[256,256]{1,0:T(8,128)}) custom-call(bf16[16,272,256]{2,1,0:T(8,128)(2,1)} %copy-done, bf16[16,256,256]{2,1,0:T(8,128)(2,1)} %copy-done.1, bf16[16,2,256,256]{3,2,1,0:T(8,128)(2,1)} %get-tuple-element.15.ty_ref, ...), custom_call_target="tpu_custom_call" | custom-call | tf_op jit(solution)/shard_map/values/pallas_call | solution.py:191
  133.1 4.5 %collective-permute-start = (f32[256,256]{1,0:T(8,128)}, f32[256,256]{1,0:T(8,128)S(1)}, u32[]{:S(2)}, u32[]{:S(2)}) collective-permute-start(f32[256,256]{1,0:T(8,128)} %get-tuple-element.22), channel_id=1, source_target_pairs={{0,16},{1,17},{2,18},{3,19},{4,20},{5,21},{6,22},{7,23},{8,24},{9,... | collective-permute-start | bytes 786440 | tf_op jit(solution)/shard_map/ppermute | solution.py:256
  137.7 1.0 copy-done.2
  138.6 14.0 %queries.1 = (f32[16,128,256]{2,1,0:T(8,128)}, f32[16,128,256]{2,1,0:T(8,128)}) custom-call(bf16[16,128,256]{2,1,0:T(8,128)(2,1)} %copy-done.2, bf16[16,272,256]{2,1,0:T(8,128)(2,1)} %copy-done, bf16[16,2,256,256]{3,2,1,0:T(8,128)(2,1)} %get-tuple-element.14.w_ref, bf16[16,2,256,256]{3,2,1,0:T(8,128)(2,1)} %get-tuple-element.17.y_ref, ...), custom_call_target="tpu_custom_call" | custom-call | tf_op jit(solution)/shard_map/queries/pallas_call | solution.py:191
  152.6 0.7 copy-done.3
  153.3 7.2 %finish.1 = bf16[16,128,256]{2,1,0:T(8,128)(2,1)} custom-call(f32[16,128,256]{2,1,0:T(8,128)} %get-tuple-element.20.o_ref, f32[16,128,256]{2,1,0:T(8,128)} %get-tuple-element.21.qt_ref, f32[256,256]{1,0:T(8,128)} %copy-done.3, f32[1,256]{1,0:T(1,128)} %bitcast.17), custom_call_target="tpu_custom_call" | custom-call | tf_op jit(solution)/shard_map/finish/pallas_call | solution.py:191
  160.6 21.3 %all_to_all.20.n_ref = bf16[16,128,256]{2,1,0:T(8,128)(2,1)} all-to-all(bf16[16,128,256]{2,1,0:T(8,128)(2,1)} %finish.1), channel_id=1, replica_groups=mesh['far'=2,'near'=4,'head'=4] {'near','head'}, dimensions={0} | all-to-all | bytes 2097152 | tf_op jit(solution)/shard_map/all_to_all | solution.py:218
  181.9 3.8 %gate.1 = bf16[128,4096]{1,0:T(8,128)(2,1)} custom-call(bf16[16,128,256]{2,1,0:T(8,128)(2,1)} %all_to_all.20.n_ref, bf16[128,4096]{1,0:T(8,128)(2,1)} %gate_ref.1), custom_call_target="tpu_custom_call" | custom-call | tf_op jit(solution)/shard_map/gate/pallas_call | solution.py:279
  (10 shorter events, 0.1 us)
Async XLA Ops:
  5.2 35.4 %all-to-all-start.2 = ((bf16[16,256,256]{2,1,0:T(8,128)(2,1)}), bf16[16,256,256]{2,1,0:T(8,128)(2,1)S(1)}, u32[]{:S(2)}, u32[]{:S(2)}) async-start(bf16[16,256,256]{2,1,0:T(8,128)(2,1)} %bitcast.12), calls=%async_computation.2 | async-start | bytes 4194304 | tf_op jit(solution)/shard_map/all_to_all | solution.py:218
  15.9 3.7 %copy-start.4 = (bf16[128,2,16]{0,2,1:T(8,128)(2,1)S(1)}, bf16[128,2,16]{0,2,1:T(8,128)(2,1)}, u32[]{:S(2)}) copy-start(bf16[128,2,16]{0,2,1:T(8,128)(2,1)} %param.9) | copy-start | bytes 24580
  40.5 1.3 copy-start.1
  41.9 35.6 %all-to-all-start.1 = ((bf16[16,272,256]{2,1,0:T(8,128)(2,1)}), bf16[16,272,256]{2,1,0:T(8,128)(2,1)S(1)}, u32[]{:S(2)}, u32[]{:S(2)}) async-start(bf16[16,272,256]{2,1,0:T(8,128)(2,1)} %pad_maximum_fusion), calls=%async_computation.1 | async-start | bytes 4456448 | tf_op jit(solution)/shard_map/all_to_all | solution.py:218
  77.5 5.7 %copy-start = (bf16[16,272,256]{2,1,0:T(8,128)(2,1)}, bf16[16,272,256]{2,1,0:T(8,128)(2,1)S(1)}, u32[]{:S(2)}) copy-start(bf16[16,272,256]{2,1,0:T(8,128)(2,1)S(1)} %all-to-all-done.1.k_ref) | copy-start | bytes 6684676
  77.5 60.2 %all-to-all-start = ((bf16[16,128,256]{2,1,0:T(8,128)(2,1)}), bf16[16,128,256]{2,1,0:T(8,128)(2,1)S(1)}, u32[]{:S(2)}, u32[]{:S(2)}) async-start(bf16[16,128,256]{2,1,0:T(8,128)(2,1)} %bitcast.14), calls=%async_computation | async-start | bytes 2097152 | tf_op jit(solution)/shard_map/all_to_all | solution.py:218
  133.1 19.5 %collective-permute-start = (f32[256,256]{1,0:T(8,128)}, f32[256,256]{1,0:T(8,128)S(1)}, u32[]{:S(2)}, u32[]{:S(2)}) collective-permute-start(f32[256,256]{1,0:T(8,128)} %get-tuple-element.22), channel_id=1, source_target_pairs={{0,16},{1,17},{2,18},{3,19},{4,20},{5,21},{6,22},{7,23},{8,24},{9,... | collective-permute-start | bytes 786440 | tf_op jit(solution)/shard_map/ppermute | solution.py:256
  137.6 1.0 copy-start.2
  152.6 0.7 copy-start.3

commit v2 on v1

v2 whole, which is shorter than its diff:
```python
import jax
import jax.numpy as jnp
from jax import lax
from jax.experimental import pallas as pl
from jax.experimental.pallas import tpu as pltpu
from jax.sharding import Mesh, PartitionSpec as P

EPS = 1e-06
F32 = jnp.float32
BF16 = jnp.bfloat16
PAD = 8
LANES = 128
PER_STEP = 4
VMEM_LIMIT = 40 << 20

NN = ((1,), (0,))
NT = ((1,), (1,))
TN = ((0,), (0,))


def dot(a, b, dims=NN):
    return lax.dot_general(a, b, (dims, ((), ())), preferred_element_type=F32)


def split(x):
    hi = x.astype(BF16)
    return hi, (x - hi.astype(F32)).astype(BF16)


def stack(parts, dims):
    axis = 1 - dims[0][0]
    return jnp.concatenate(parts, axis=axis), parts[0].shape[axis]


def dot3(a, b, dims=NN):
    both, rows = stack(a, dims)
    top = dot(both, b[0], dims)
    return top[:rows] + top[rows:] + dot(a[0], b[1], dims)


def dot2r(a, b, dims=NN):
    return dot(a, b[0], dims) + dot(a, b[1], dims)


def dot2l(a, b, dims=NN):
    both, rows = stack(a, dims)
    top = dot(both, b, dims)
    return top[:rows] + top[rows:]


def put(ref, i, parts):
    ref[i, 0] = parts[0]
    ref[i, 1] = parts[1]


def get(ref, i):
    return ref[i, 0], ref[i, 1]


def interleave(even, odd, size):
    pieces = []
    for i in range(0, even.shape[0], size):
        pieces += [even[i : i + size], odd[i : i + size]]
    return jnp.concatenate(pieces, axis=0)


def take(x, size, start):
    return jnp.concatenate(
        [x[i : i + size] for i in range(start, x.shape[0], 2 * size)], axis=0
    )


def block_inverses(grams, g_rows):
    n = grams[0].shape[0]
    row = lax.broadcasted_iota(jnp.int32, (n, n), 0)
    col = lax.broadcasted_iota(jnp.int32, (n, n), 1)
    pair = (row // 2 == col // 2) & (row > col)
    out = []
    for gram, g_row in zip(grams, g_rows):
        diag = jnp.where(row == col, g_row, 0.0)
        g_col = jnp.sum(diag, axis=1, keepdims=True)
        out.append(diag - jnp.where(pair, g_col * (gram * g_row), 0.0))
    parts = [split(gram) for gram in grams]
    size = 2
    while size < n:
        sp = [split(t) for t in out]
        if size < 8:
            mask = (row // (2 * size) == col // (2 * size)) & (row // size > col // size)
            mid = [split(jnp.where(mask, dot3(t, p), 0.0)) for t, p in zip(sp, parts)]
            out = [t - dot3(m, s) for t, m, s in zip(out, mid, sp)]
        else:
            r = lax.broadcasted_iota(jnp.int32, (n // 2, n), 0)
            c = lax.broadcasted_iota(jnp.int32, (n // 2, n), 1)
            mask = c // size == 2 * (r // size)
            odd = [take(t, size, size) for t in out]
            mid = [split(jnp.where(mask, dot3(split(o), p), 0.0)) for o, p in zip(odd, parts)]
            low = [o - dot3(m, s) for o, m, s in zip(odd, mid, sp)]
            out = [interleave(take(t, size, 0), l, size) for t, l in zip(out, low)]
        size *= 2
    return out


def inverses(grams, g_rows):
    n = grams[0].shape[0]
    if n <= LANES:
        return block_inverses(grams, g_rows)
    h = n // 2
    both = inverses(
        [g[:h, :h] for g in grams] + [g[h:, h:] for g in grams],
        [g[:, :h] for g in g_rows] + [g[:, h:] for g in g_rows],
    )
    out = []
    for gram, t1, t2 in zip(grams, both[: len(grams)], both[len(grams) :]):
        mid = dot3(split(gram[h:, :h]), split(t1))
        low = -dot3(split(t2), split(mid))
        out.append(
            jnp.concatenate(
                [
                    jnp.concatenate([t1, jnp.zeros_like(t1)], axis=1),
                    jnp.concatenate([low, t2], axis=1),
                ],
                axis=0,
            )
        )
    return out


def eye(n):
    row = lax.broadcasted_iota(jnp.int32, (n, n), 0)
    return row == lax.broadcasted_iota(jnp.int32, (n, n), 1)


def keys_kernel(k_ref, t_ref, n_ref, rt_ref, e_ref, fin_ref, state):
    per, _, steps, width = t_ref.shape

    @pl.when(pl.program_id(0) == 0)
    def _():
        state[...] = jnp.where(eye(width), 1.0, 0.0)

    diag = eye(steps)
    ks = [k_ref[i, :steps] for i in range(per)]
    grams = [dot(k, k, NT) for k in ks]
    squares = [jnp.where(diag, g, 0.0) for g in grams]
    sq = [jnp.sum(s, axis=0, keepdims=True) + EPS for s in squares]
    n_cols = [jnp.sqrt(jnp.sum(s, axis=1, keepdims=True) + EPS) for s in squares]
    g_rows = [k_ref[i, steps:].astype(F32)[0:1] / s for i, s in enumerate(sq)]
    ts = [split(t) for t in inverses(grams, g_rows)]
    ws = [split(dot2l(t, k)) for t, k in zip(ts, ks)]
    rts = [split(dot2l(w, k, TN)) for k, w in zip(ks, ws)]
    for i in range(per):
        put(t_ref, i, ts[i])
        n_ref[i] = jnp.broadcast_to(jnp.sqrt(sq[i]), n_ref.shape[1:])
        put(rt_ref, i, rts[i])
    f = state[...]
    for i in reversed(range(per)):
        parts = split(f)
        f = f - dot3(rts[i], parts)
        e = dot3(ts[i], split(dot2r(ks[i], parts)), TN)
        put(e_ref, i, split(n_cols[i] * e))
    state[...] = f
    fin_ref[...] = f


def ends_kernel(v_ref, e_ref, fin_ref):
    per = v_ref.shape[0]

    @pl.when(pl.program_id(0) == 0)
    def _():
        fin_ref[...] = jnp.zeros_like(fin_ref)

    total = fin_ref[...]
    for i in range(per):
        total = total + dot2r(v_ref[i], get(e_ref, i), TN)
    fin_ref[...] = total


def local_kernel(q_ref, k_ref, v_ref, t_ref, n_ref, rt_ref, o_ref, qt_ref, state_a, state_b):
    per, toks, width = q_ref.shape
    steps = v_ref.shape[1]
    refl = steps // toks

    @pl.when(pl.program_id(0) == 0)
    def _():
        state_a[...] = jnp.where(eye(width), 1.0, 0.0)
        state_b[...] = jnp.zeros_like(state_b)

    tok = lax.broadcasted_iota(jnp.int32, (toks, steps), 0)
    step = lax.broadcasted_iota(jnp.int32, (toks, steps), 1)
    causal = step // refl <= tok
    a, b = state_a[...], state_b[...]
    for i in range(per):
        q, k, v = q_ref[i], k_ref[i, :steps], v_ref[i]
        t, rt, n_row = get(t_ref, i), get(rt_ref, i), n_ref[i, 0:1]
        qf = q.astype(F32)
        inv = 1.0 / jnp.sqrt(jnp.sum(qf * qf, axis=1, keepdims=True) + EPS)
        s = split(jnp.where(causal, dot(q, k, NT), 0.0))
        st = dot3(s, t)
        qw = split(inv * (qf - dot2l(split(st), k)))
        near = dot2l(split(inv * (st * n_row)), v)
        y = split(dot2l(split((t[0].astype(F32) + t[1].astype(F32)) * n_row), v))
        bt = dot2l(y, k, TN)
        pa, pb = split(a), split(b)
        o_ref[i] = near + dot3(qw, pb, NT)
        put(qt_ref, i, split(dot3(qw, pa, NT)))
        a = a - dot3(pa, rt)
        b = b + (bt - dot3(pb, rt))
    state_a[...] = a
    state_b[...] = b


def finish_kernel(o_ref, qt_ref, s_ref, gain_ref, out_ref):
    s = split(s_ref[...])
    for i in range(o_ref.shape[0]):
        o = o_ref[i] + dot3(get(qt_ref, i), s, NT)
        mean = jnp.mean(o * o, axis=1, keepdims=True)
        out_ref[i] = (o * lax.rsqrt(mean + EPS) * gain_ref[...]).astype(BF16)


def gate_kernel(n_ref, gate_ref, out_ref):
    per, _, width = n_ref.shape
    for i in range(per):
        g = gate_ref[:, i * width : (i + 1) * width].astype(F32)
        out_ref[:, i * width : (i + 1) * width] = (
            n_ref[i].astype(F32) * (g / (1.0 + jnp.exp(-g)))
        ).astype(BF16)


def steps_kernel(x_ref, *rest):
    out_ref = rest[-1]
    per = out_ref.shape[0]
    toks, refl, wide = x_ref.shape
    width = wide // per
    steps = toks * refl
    for i in range(per):
        out_ref[i, :steps] = x_ref[:, :, i * width : (i + 1) * width].reshape(steps, width)
        if len(rest) > 1:
            out_ref[i, steps:] = rest[0][i]


def rows_kernel(x_ref, out_ref):
    per, _, width = out_ref.shape
    for i in range(per):
        out_ref[i] = x_ref[:, i * width : (i + 1) * width]


def params():
    return pltpu.CompilerParams(
        dimension_semantics=("arbitrary",), vmem_limit_bytes=VMEM_LIMIT
    )


def call(kernel, grid, ins, outs, scratch=(), backward=False):
    def spec(a, per):
        zeros = (0,) * (len(a.shape) - 1)
        if per is None:
            return pl.BlockSpec(a.shape, lambda c: (0,) + zeros)
        if backward:
            return pl.BlockSpec((per,) + a.shape[1:], lambda c: (grid - 1 - c,) + zeros)
        return pl.BlockSpec((per,) + a.shape[1:], lambda c: (c,) + zeros)

    return pl.pallas_call(
        kernel,
        grid=(grid,),
        in_specs=[spec(*i) for i in ins],
        out_specs=[spec(*o) for o in outs],
        out_shape=[o[0] for o in outs],
        scratch_shapes=list(scratch),
        compiler_params=params(),
    )(*[i[0] for i in ins])


def by_head(x, width, extra=None, per=4):
    heads = x.shape[-1] // width
    lead = x.shape[:-1]
    rows = lead[0] * (lead[1] if len(lead) > 1 else 1)
    total = rows + (extra.shape[1] if extra is not None else 0)
    zeros = (0,) * len(lead)
    specs = [pl.BlockSpec(lead + (per * width,), lambda c: zeros + (c,))]
    args = [x]
    if extra is not None:
        specs.append(pl.BlockSpec((per,) + extra.shape[1:], lambda c: (c, 0, 0)))
        args.append(extra)
    return pl.pallas_call(
        steps_kernel if len(lead) > 1 else rows_kernel,
        grid=(heads // per,),
        in_specs=specs,
        out_specs=pl.BlockSpec((per, total, width), lambda c: (c, 0, 0)),
        out_shape=jax.ShapeDtypeStruct((heads, total, width), x.dtype),
        name="by_head",
        compiler_params=params(),
    )(*args)


def shards(queries, keys, values, betas, gate, norm_gain):
    toks, refl = keys.shape[:2]
    width = norm_gain.shape[0]
    heads = queries.shape[1] // width
    steps = toks * refl
    near = ("near", "head")
    far_size = lax.axis_size("far")
    blocks = lax.axis_size("near") * lax.axis_size("head")

    def exchange(x):
        return lax.all_to_all(x, near, 0, 0, tiled=True)

    b_rows = jnp.broadcast_to(betas.reshape(steps, heads).T[:, None, :], (heads, PAD, steps))
    k = exchange(by_head(keys, width, b_rows))
    v_out, q_out = by_head(values, width), by_head(queries, width, per=8)
    v = exchange(v_out)

    per = PER_STEP
    grid = blocks // per
    sds = jax.ShapeDtypeStruct
    square = sds((blocks, 2, width, width), BF16)
    state = sds((width, width), F32)
    keep = pltpu.VMEM((width, width), F32)
    t, n, rt, e, end_a = call(
        keys_kernel,
        grid,
        [(k, per)],
        [
            (sds((blocks, 2, steps, steps), BF16), per),
            (sds((blocks, 8, steps), F32), per),
            (square, per),
            (sds((blocks, 2, steps, width), BF16), per),
            (state, None),
        ],
        (keep,),
        backward=True,
    )
    q = exchange(q_out)
    (end_b,) = call(ends_kernel, grid, [(v, per), (e, per)], [(state, None)], ())
    route = [(i, i + 1) for i in range(far_size - 1)]
    start = lax.ppermute(end_b, "far", route)
    for _ in range(far_size - 2):
        sent = jnp.dot(start, end_a, precision=lax.Precision.HIGHEST) + end_b
        start = lax.ppermute(sent, "far", route)
    o, qt = call(
        local_kernel,
        grid,
        [(q, per), (k, per), (v, per), (t, per), (n, per), (rt, per)],
        [(sds((blocks, toks, width), F32), per), (sds((blocks, 2, toks, width), BF16), per)],
        (keep, keep),
    )
    (normed,) = call(
        finish_kernel,
        grid,
        [(o, per), (qt, per), (start, None), (norm_gain[None, :], None)],
        [(sds((blocks, toks, width), BF16), per)],
        (),
    )
    normed = exchange(normed)
    wide = 4
    return pl.pallas_call(
        gate_kernel,
        grid=(heads // wide,),
        in_specs=[
            pl.BlockSpec((wide, toks, width), lambda c: (c, 0, 0)),
            pl.BlockSpec((toks, wide * width), lambda c: (0, c)),
        ],
        out_specs=pl.BlockSpec((toks, wide * width), lambda c: (0, c)),
        out_shape=sds((toks, heads * width), BF16),
        name="gate",
        compiler_params=params(),
    )(normed, gate)


def solution(mesh):
    def step(queries, keys, values, betas, gate, norm_gain):
        heads = queries.shape[1] // norm_gain.shape[0]
        seq, head = mesh.shape["seq"], mesh.shape["head"]
        near = heads // head
        fine = Mesh(mesh.devices.reshape(seq // near, near, head), ("far", "near", "head"))
        lead = ("far", "near", "head")
        placed = (
            P(lead, None),
            P(lead, None, None),
            P(lead, None, None),
            P(lead, None, None),
            P(lead, None),
            P(),
        )

        run = jax.shard_map(
            shards, mesh=fine, in_specs=placed, out_specs=P(lead, None), check_vma=False
        )
        return run(queries, keys, values, betas, gate, norm_gain)

    return step
```

time: 187 us -> 163 us (0.87)
  Pallas kernels: 75 us -> 47.9 us
  waiting for transfers between devices: 45.4 us -> 53.8 us
  other arithmetic: 3.11 us -> 0 us
    pallas_call x4, Pallas kernels: 71.1 us -> 43.2 us  [call(): pl.pallas_call(kernel, grid=(grid,), in_specs=[spec(*i) for i in ins], ou...]
    reshape x5 -> x0, local copies, waits for them, and re-layouts: 14.5 us -> none  [by_head(): return x.reshape(rows, heads, width).transpose(1, 0, 2)]
    unnamed x12 -> x35, local copies, waits for them, and re-layouts: 4.74 us -> 18.1 us
    all_to_all x3, waiting for transfers between devices: 45.4 us -> 53.8 us  [exchange(): return lax.all_to_all(x, near, 0, 0, tiled=True)]
    concatenate x1 -> x0, other arithmetic: 3.11 us -> none  [shards(): k = exchange(jnp.concatenate([by_head(keys, steps), b_rows], axis=1))]
    pallas_call x0 -> x3, Pallas kernels: none -> 2.63 us  [by_head(): pl.pallas_call(steps_kernel if len(lead) > 1 else rows_kernel, grid=(head...]
  transfers between devices with their start and end apart: 4 -> 4, of which waited for: 2 -> 2; matrix products, arithmetic and copies ran while one was open for 8% -> 0% of each run, Pallas kernels for 34% -> 26%
where the time goes in v2:
time: 163 us
  waiting for transfers between devices  53.8 us (33%)
  Pallas kernels  47.9 us (29%)
  starting transfers between devices  21.2 us (13%)
  blocking collectives  21.2 us (13%)
  local copies, waits for them, and re-layouts  18.2 us (11%)
    all_to_all x3, waiting for transfers between devices, exchange(): return lax.all_to_all(x, near, 0, 0, tiled=True)  53.8 us
    pallas_call x4, Pallas kernels, call(): pl.pallas_call(kernel, grid=(grid,), in_specs=[spec(*i) for i in ins], ou...  43.2 us
    all_to_all x1, blocking collectives, exchange(): return lax.all_to_all(x, near, 0, 0, tiled=True)  21.2 us
    unnamed x35, local copies, waits for them, and re-layouts  18.1 us
    all_to_all x3, starting transfers between devices, exchange(): return lax.all_to_all(x, near, 0, 0, tiled=True)  16.7 us
    ppermute x1, starting transfers between devices, shards(): start = lax.ppermute(end_b, 'far', route)  4.5 us
  transfers between devices with their start and end apart: 4, of which 2 were waited for; matrix products, arithmetic and copies ran while one was open for 0% of the time, Pallas kernels for 26%

profile of v2, /device:TPU:0, one launch (start us, length us, event | category | flops | bytes accessed | tf_op | source)
XLA Modules:
  0.0 162.5 jit_solution(3828337910145908346)
XLA Ops:
  0.0 1.6 copy-done.9
  2.4 1.3 copy-done.4
  3.7 6.4 %all-to-all-start.2 = ((bf16[16,256,256]{2,1,0:T(8,128)(2,1)}), bf16[16,256,256]{2,1,0:T(8,128)(2,1)S(1)}, u32[]{:S(2)}, u32[]{:S(2)}) async-start(bf16[16,256,256]{2,1,0:T(8,128)(2,1)} %copy-done.4), calls=%async_computation.2 | async-start | bytes 4194304 | tf_op jit(solution)/shard_map/all_to_all | solution.py:304
  10.4 1.6 copy-done.10
  12.7 1.3 copy-done.3
  14.1 25.1 %all-to-all-done.2.v_ref = bf16[16,256,256]{2,1,0:T(8,128)(2,1)S(1)} async-done(((bf16[16,256,256]{2,1,0:T(8,128)(2,1)}), bf16[16,256,256]{2,1,0:T(8,128)(2,1)S(1)}, u32[]{:S(2)}, u32[]{:S(2)}) %all-to-all-start.2) | async-done | bytes 2097184 | tf_op jit(solution)/shard_map/all_to_all | solution.py:304
  39.2 1.3 copy-done
  40.5 4.9 %all-to-all-start.1 = ((bf16[16,264,256]{2,1,0:T(8,128)(2,1)}), bf16[16,264,256]{2,1,0:T(8,128)(2,1)S(1)}, u32[]{:S(2)}, u32[]{:S(2)}) async-start(bf16[16,264,256]{2,1,0:T(8,128)(2,1)} %copy-done.3), calls=%async_computation.1 | async-start | bytes 4325376 | tf_op jit(solution)/shard_map/all_to_all | solution.py:304
  45.4 1.1 by_head.3
  46.5 28.7 %all-to-all-done.1.k_ref = bf16[16,264,256]{2,1,0:T(8,128)(2,1)S(1)} async-done(((bf16[16,264,256]{2,1,0:T(8,128)(2,1)}), bf16[16,264,256]{2,1,0:T(8,128)(2,1)S(1)}, u32[]{:S(2)}, u32[]{:S(2)}) %all-to-all-start.1) | async-done | bytes 2162720 | tf_op jit(solution)/shard_map/all_to_all | solution.py:304
  75.3 5.4 %all-to-all-start = ((bf16[16,128,256]{2,1,0:T(8,128)(2,1)}), bf16[16,128,256]{2,1,0:T(8,128)(2,1)S(1)}, u32[]{:S(2)}, u32[]{:S(2)}) async-start(bf16[16,128,256]{2,1,0:T(8,128)(2,1)} %by_head.3), calls=%async_computation | async-start | bytes 2097152 | tf_op jit(solution)/shard_map/all_to_all | solution.py:304
  80.7 22.7 %shard_map.64 = (bf16[16,2,256,256]{3,2,1,0:T(8,128)(2,1)S(1)}, f32[16,8,256]{2,1,0:T(8,128)S(1)}, bf16[16,2,256,256]{3,2,1,0:T(8,128)(2,1)S(1)}, bf16[16,2,256,256]{3,2,1,0:T(8,128)(2,1)}, f32[256,256]{1,0:T(8,128)}) custom-call(bf16[16,264,256]{2,1,0:T(8,128)(2,1)S(1)} %all-to-all-done.1.k_ref), custom_call_target="tpu_custom_call" | custom-call | tf_op jit(solution)/shard_map/pallas_call | solution.py:261
  103.3 2.0 %copy-done.5 = bf16[16,2,256,256]{3,2,1,0:T(8,128)(2,1)} copy-done((bf16[16,2,256,256]{3,2,1,0:T(8,128)(2,1)}, bf16[16,2,256,256]{3,2,1,0:T(8,128)(2,1)S(1)}, u32[]{:S(2)}) %copy-start.5) | copy-done | bytes 4194328
  105.4 1.9 %copy-done.7 = bf16[16,2,256,256]{3,2,1,0:T(8,128)(2,1)} copy-done((bf16[16,2,256,256]{3,2,1,0:T(8,128)(2,1)}, bf16[16,2,256,256]{3,2,1,0:T(8,128)(2,1)S(1)}, u32[]{:S(2)}) %copy-start.7) | copy-done | bytes 4194328
  107.3 2.2 %copy-done.8 = bf16[16,2,256,256]{3,2,1,0:T(8,128)(2,1)S(1)} copy-done((bf16[16,2,256,256]{3,2,1,0:T(8,128)(2,1)S(1)}, bf16[16,2,256,256]{3,2,1,0:T(8,128)(2,1)}, u32[]{:S(2)}) %copy-start.8) | copy-done | bytes 4194328
  109.5 2.7 %shard_map.66 = f32[256,256]{1,0:T(8,128)} custom-call(bf16[16,256,256]{2,1,0:T(8,128)(2,1)S(1)} %copy-done.1, bf16[16,2,256,256]{3,2,1,0:T(8,128)(2,1)S(1)} %copy-done.8), custom_call_target="tpu_custom_call" | custom-call | tf_op jit(solution)/shard_map/pallas_call | solution.py:261
  112.2 4.5 %collective-permute-start = (f32[256,256]{1,0:T(8,128)}, f32[256,256]{1,0:T(8,128)S(1)}, u32[]{:S(2)}, u32[]{:S(2)}) collective-permute-start(f32[256,256]{1,0:T(8,128)} %shard_map.66), channel_id=1, source_target_pairs={{0,16},{1,17},{2,18},{3,19},{4,20},{5,21},{6,22},{7,23},{8,24},{9,... | collective-permute-start | bytes 786440 | tf_op jit(solution)/shard_map/ppermute | solution.py:334
  116.7 1.6 copy-done.2
  118.3 2.2 %copy-done.6 = bf16[16,2,256,256]{3,2,1,0:T(8,128)(2,1)S(1)} copy-done((bf16[16,2,256,256]{3,2,1,0:T(8,128)(2,1)S(1)}, bf16[16,2,256,256]{3,2,1,0:T(8,128)(2,1)}, u32[]{:S(2)}) %copy-start.6) | copy-done | bytes 4194328
  120.5 0.9 copy-done.14
  121.4 15.7 %shard_map.65 = (f32[16,128,256]{2,1,0:T(8,128)S(1)}, bf16[16,2,128,256]{3,2,1,0:T(8,128)(2,1)S(1)}) custom-call(bf16[16,128,256]{2,1,0:T(8,128)(2,1)S(1)} %all-to-all-done.q_ref, bf16[16,264,256]{2,1,0:T(8,128)(2,1)S(1)} %all-to-all-done.1.k_ref, bf16[16,256,256]{2,1,0:T(8,128)(2,1)S(1)} %copy-done.2, bf16[16,2,256,256]{3,2,1,0:T(8,128)(2,1)S(1)} %copy-done.6, ...), custom_call_target="tpu_custom_call" | custom-call | tf_op jit(solution)/shard_map/pallas_call | solution.py:261
  137.1 2.2 %shard_map.67 = bf16[16,128,256]{2,1,0:T(8,128)(2,1)S(1)} custom-call(f32[16,128,256]{2,1,0:T(8,128)S(1)} %get-tuple-element.14.o_ref, bf16[16,2,128,256]{3,2,1,0:T(8,128)(2,1)S(1)} %get-tuple-element.15.qt_ref, f32[256,256]{1,0:T(8,128)S(1)} %collective-permute-done.s_ref, f32[1,256]{1,0:T(1,128)S(1)} %bitcast.4), custom_call_target="tpu_custom_call" | custom-call | tf_op jit(solution)/shard_map/pallas_call | solution.py:261
  139.4 21.2 %all_to_all.20.n_ref = bf16[16,128,256]{2,1,0:T(8,128)(2,1)S(1)} all-to-all(bf16[16,128,256]{2,1,0:T(8,128)(2,1)S(1)} %shard_map.67), channel_id=1, replica_groups=mesh['far'=2,'near'=4,'head'=4] {'near','head'}, dimensions={0} | all-to-all | bytes 2097152 | tf_op jit(solution)/shard_map/all_to_all | solution.py:304
  160.5 2.0 %gate.1 = bf16[128,4096]{1,0:T(8,128)(2,1)} custom-call(bf16[16,128,256]{2,1,0:T(8,128)(2,1)S(1)} %all_to_all.20.n_ref, bf16[128,4096]{1,0:T(8,128)(2,1)S(1)} %copy-done.11), custom_call_target="tpu_custom_call" | custom-call | tf_op jit(solution)/shard_map/gate/pallas_call | solution.py:354
  (30 shorter events, 1.8 us)
Async XLA Ops:
  0.0 1.6 copy-start.9
  2.4 1.3 copy-start.4
  3.7 6.5 %copy-start.16 = (bf16[128,2,16]{0,2,1:T(8,128)(2,1)S(1)}, bf16[128,2,16]{0,2,1:T(8,128)(2,1)}, u32[]{:S(2)}) copy-start(bf16[128,2,16]{0,2,1:T(8,128)(2,1)} %param.9) | copy-start | bytes 24580
  3.7 35.5 %all-to-all-start.2 = ((bf16[16,256,256]{2,1,0:T(8,128)(2,1)}), bf16[16,256,256]{2,1,0:T(8,128)(2,1)S(1)}, u32[]{:S(2)}, u32[]{:S(2)}) async-start(bf16[16,256,256]{2,1,0:T(8,128)(2,1)} %copy-done.4), calls=%async_computation.2 | async-start | bytes 4194304 | tf_op jit(solution)/shard_map/all_to_all | solution.py:304
  10.4 1.6 copy-start.10
  12.7 1.4 copy-start.3
  14.1 31.3 %copy-start.12 = (bf16[128,4096]{1,0:T(8,128)(2,1)S(1)}, bf16[128,4096]{1,0:T(8,128)(2,1)}, u32[]{:S(2)}) copy-start(bf16[128,4096]{1,0:T(8,128)(2,1)} %x_ref.3) | copy-start | bytes 3145732
  39.2 1.3 copy-start
  40.5 34.8 %all-to-all-start.1 = ((bf16[16,264,256]{2,1,0:T(8,128)(2,1)}), bf16[16,264,256]{2,1,0:T(8,128)(2,1)S(1)}, u32[]{:S(2)}, u32[]{:S(2)}) async-start(bf16[16,264,256]{2,1,0:T(8,128)(2,1)} %copy-done.3), calls=%async_computation.1 | async-start | bytes 4325376 | tf_op jit(solution)/shard_map/all_to_all | solution.py:304
  75.3 41.4 %all-to-all-start = ((bf16[16,128,256]{2,1,0:T(8,128)(2,1)}), bf16[16,128,256]{2,1,0:T(8,128)(2,1)S(1)}, u32[]{:S(2)}, u32[]{:S(2)}) async-start(bf16[16,128,256]{2,1,0:T(8,128)(2,1)} %by_head.3), calls=%async_computation | async-start | bytes 2097152 | tf_op jit(solution)/shard_map/all_to_all | solution.py:304
  80.7 26.6 %copy-start.1 = (bf16[16,256,256]{2,1,0:T(8,128)(2,1)S(1)}, bf16[16,256,256]{2,1,0:T(8,128)(2,1)}, u32[]{:S(2)}) copy-start(bf16[16,256,256]{2,1,0:T(8,128)(2,1)} %copy-done) | copy-start | bytes 6291460
  103.3 2.0 %copy-start.5 = (bf16[16,2,256,256]{3,2,1,0:T(8,128)(2,1)}, bf16[16,2,256,256]{3,2,1,0:T(8,128)(2,1)S(1)}, u32[]{:S(2)}) copy-start(bf16[16,2,256,256]{3,2,1,0:T(8,128)(2,1)S(1)} %get-tuple-element.11.t_ref) | copy-start | bytes 12582916
  105.4 1.9 %copy-start.7 = (bf16[16,2,256,256]{3,2,1,0:T(8,128)(2,1)}, bf16[16,2,256,256]{3,2,1,0:T(8,128)(2,1)S(1)}, u32[]{:S(2)}) copy-start(bf16[16,2,256,256]{3,2,1,0:T(8,128)(2,1)S(1)} %get-tuple-element.13.rt_ref) | copy-start | bytes 12582916
  107.3 4.9 %copy-start.13 = (f32[16,8,256]{2,1,0:T(8,128)}, f32[16,8,256]{2,1,0:T(8,128)S(1)}, u32[]{:S(2)}) copy-start(f32[16,8,256]{2,1,0:T(8,128)S(1)} %get-tuple-element.12.n_ref) | copy-start | bytes 393220
  107.3 2.2 %copy-start.8 = (bf16[16,2,256,256]{3,2,1,0:T(8,128)(2,1)S(1)}, bf16[16,2,256,256]{3,2,1,0:T(8,128)(2,1)}, u32[]{:S(2)}) copy-start(bf16[16,2,256,256]{3,2,1,0:T(8,128)(2,1)} %get-tuple-element.16.e_ref) | copy-start | bytes 12582916
  112.2 24.9 %collective-permute-start = (f32[256,256]{1,0:T(8,128)}, f32[256,256]{1,0:T(8,128)S(1)}, u32[]{:S(2)}, u32[]{:S(2)}) collective-permute-start(f32[256,256]{1,0:T(8,128)} %shard_map.66), channel_id=1, source_target_pairs={{0,16},{1,17},{2,18},{3,19},{4,20},{5,21},{6,22},{7,23},{8,24},{9,... | collective-permute-start | bytes 786440 | tf_op jit(solution)/shard_map/ppermute | solution.py:334
  116.7 1.6 copy-start.2
  118.3 2.2 %copy-start.6 = (bf16[16,2,256,256]{3,2,1,0:T(8,128)(2,1)S(1)}, bf16[16,2,256,256]{3,2,1,0:T(8,128)(2,1)}, u32[]{:S(2)}) copy-start(bf16[16,2,256,256]{3,2,1,0:T(8,128)(2,1)} %copy-done.5) | copy-start | bytes 12582916
  120.5 0.9 copy-start.14
  121.4 15.7 %copy-start.15 = (f32[256]{0:T(256)S(1)}, f32[256]{0:T(256)}, u32[]{:S(2)}) copy-start(f32[256]{0:T(256)} %param.11) | copy-start | bytes 3076
  139.3 21.2 %copy-start.11 = (bf16[128,4096]{1,0:T(8,128)(2,1)S(1)}, bf16[128,4096]{1,0:T(8,128)(2,1)}, u32[]{:S(2)}) copy-start(bf16[128,4096]{1,0:T(8,128)(2,1)} %gate_ref.1) | copy-start | bytes 3145732

commit v3 on v2

--- a/solution.py
+++ b/solution.py
@@ -1,3 +1,5 @@
+import functools
+
 import jax
 import jax.numpy as jnp
 from jax import lax
@@ -75,13 +77,19 @@
     row = lax.broadcasted_iota(jnp.int32, (n, n), 0)
     col = lax.broadcasted_iota(jnp.int32, (n, n), 1)
     pair = (row // 2 == col // 2) & (row > col)
+    quad = (row // 4 == col // 4) & (row // 2 > col // 2)
     out = []
     for gram, g_row in zip(grams, g_rows):
         diag = jnp.where(row == col, g_row, 0.0)
         g_col = jnp.sum(diag, axis=1, keepdims=True)
-        out.append(diag - jnp.where(pair, g_col * (gram * g_row), 0.0))
+        sub = jnp.where(pair, g_col * (gram * g_row), 0.0)
+        s_col = jnp.sum(sub, axis=1, keepdims=True)
+        s_row = jnp.sum(sub, axis=0, keepdims=True)
+        mid = g_col * gram - s_col * pltpu.roll(gram, 1, 0)
+        low = mid * g_row - pltpu.roll(mid, n - 1, 1) * s_row
+        out.append(diag - sub - jnp.where(quad, low, 0.0))
     parts = [split(gram) for gram in grams]
-    size = 2
+    size = 4
     while size < n:
         sp = [split(t) for t in out]
         if size < 8:
@@ -130,51 +138,79 @@
     return row == lax.broadcasted_iota(jnp.int32, (n, n), 1)
 
 
-def keys_kernel(k_ref, t_ref, n_ref, rt_ref, e_ref, fin_ref, state):
+def keys_kernel(k_ref, t_ref, n_ref, r_ref, e_ref, fin_ref, state, k_s, t_s, r_s, n_s):
     per, _, steps, width = t_ref.shape
-
-    @pl.when(pl.program_id(0) == 0)
+    now = pl.program_id(0)
+    last = pl.num_programs(0) - 1
+    slot = now % 2
+
+    @pl.when(now == 0)
     def _():
         state[...] = jnp.where(eye(width), 1.0, 0.0)
 
-    diag = eye(steps)
-    ks = [k_ref[i, :steps] for i in range(per)]
-    grams = [dot(k, k, NT) for k in ks]
-    squares = [jnp.where(diag, g, 0.0) for g in grams]
-    sq = [jnp.sum(s, axis=0, keepdims=True) + EPS for s in squares]
-    n_cols = [jnp.sqrt(jnp.sum(s, axis=1, keepdims=True) + EPS) for s in squares]
-    g_rows = [k_ref[i, steps:].astype(F32)[0:1] / s for i, s in enumerate(sq)]
-    ts = [split(t) for t in inverses(grams, g_rows)]
-    ws = [split(dot2l(t, k)) for t, k in zip(ts, ks)]
-    rts = [split(dot2l(w, k, TN)) for k, w in zip(ks, ws)]
-    for i in range(per):
-        put(t_ref, i, ts[i])
-        n_ref[i] = jnp.broadcast_to(jnp.sqrt(sq[i]), n_ref.shape[1:])
-        put(rt_ref, i, rts[i])
-    f = state[...]
-    for i in reversed(range(per)):
-        parts = split(f)
-        f = f - dot3(rts[i], parts)
-        e = dot3(ts[i], split(dot2r(ks[i], parts)), TN)
-        put(e_ref, i, split(n_cols[i] * e))
-    state[...] = f
-    fin_ref[...] = f
-
-
-def ends_kernel(v_ref, e_ref, fin_ref):
-    per = v_ref.shape[0]
-
-    @pl.when(pl.program_id(0) == 0)
+    def front():
+        diag = eye(steps)
+        ks = [k_ref[i, :steps] for i in range(per)]
+        grams = [dot(k, k, NT) for k in ks]
+        squares = [jnp.where(diag, g, 0.0) for g in grams]
+        sq = [jnp.sum(s, axis=0, keepdims=True) + EPS for s in squares]
+        g_rows = [k_ref[i, steps:].astype(F32)[0:1] / s for i, s in enumerate(sq)]
+        ts = [split(t) for t in inverses(grams, g_rows)]
+        ws = [split(dot2l(t, k)) for t, k in zip(ts, ks)]
+        rs = [split(dot2r(k, w, TN)) for k, w in zip(ks, ws)]
+        for i in range(per):
+            n_row = jnp.sqrt(sq[i])
+            n_s[slot, i] = n_row
+            n_ref[i] = jnp.broadcast_to(n_row, n_ref.shape[1:])
+            k_s[slot, i] = ks[i]
+            for j in range(2):
+                t_s[slot, i, j] = ts[i][j]
+                r_s[slot, i, j] = rs[i][j]
+            put(t_ref, i, ts[i])
+            put(r_ref, i, rs[i])
+
+    def chain():
+        f = state[...]
+        for i in reversed(range(per)):
+            r = r_s[1 - slot, i, 0], r_s[1 - slot, i, 1]
+            t = t_s[1 - slot, i, 0], t_s[1 - slot, i, 1]
+            parts = split(f)
+            f = f - dot3(parts, r)
+            e = dot3(split(dot2l(parts, k_s[1 - slot, i], NT)), t)
+            put(e_ref, i, split(e * n_s[1 - slot, i]))
+        f = jnp.where(now > 0, f, state[...])
+        state[...] = f
+        fin_ref[...] = f
+
+    @pl.when(now < last)
     def _():
-        fin_ref[...] = jnp.zeros_like(fin_ref)
-
-    total = fin_ref[...]
-    for i in range(per):
-        total = total + dot2r(v_ref[i], get(e_ref, i), TN)
-    fin_ref[...] = total
-
-
-def local_kernel(q_ref, k_ref, v_ref, t_ref, n_ref, rt_ref, o_ref, qt_ref, state_a, state_b):
+        chain()
+        front()
+
+    @pl.when(now == last)
+    def _():
+        chain()
+
+
+def ends_kernel(me_ref, e_ref, *refs, per):
+    v_out_ref, fin_ref = refs[-2:]
+    step = pl.program_id(0)
+    within = me_ref[0] % per
+    for g in range((len(refs) - 2) // per):
+
+        @pl.when(step == g)
+        def _():
+            total = None if g == 0 else fin_ref[...]
+            for d in range(per):
+                c = within ^ d
+                v = refs[g * per + d][...]
+                v_out_ref[c] = v
+                term = dot2l(get(e_ref, c), v)
+                total = term if total is None else total + term
+            fin_ref[...] = total
+
+
+def local_kernel(q_ref, k_ref, v_ref, t_ref, n_ref, r_ref, o_ref, qt_ref, state_a, state_b):
     per, toks, width = q_ref.shape
     steps = v_ref.shape[1]
     refl = steps // toks
@@ -190,20 +226,20 @@
     a, b = state_a[...], state_b[...]
     for i in range(per):
         q, k, v = q_ref[i], k_ref[i, :steps], v_ref[i]
-        t, rt, n_row = get(t_ref, i), get(rt_ref, i), n_ref[i, 0:1]
+        t, r, n_row = get(t_ref, i), get(r_ref, i), n_ref[i, 0:1]
         qf = q.astype(F32)
         inv = 1.0 / jnp.sqrt(jnp.sum(qf * qf, axis=1, keepdims=True) + EPS)
         s = split(jnp.where(causal, dot(q, k, NT), 0.0))
         st = dot3(s, t)
         qw = split(inv * (qf - dot2l(split(st), k)))
         near = dot2l(split(inv * (st * n_row)), v)
-        y = split(dot2l(split((t[0].astype(F32) + t[1].astype(F32)) * n_row), v))
-        bt = dot2l(y, k, TN)
+        ty = split((t[0].astype(F32) + t[1].astype(F32)) * n_row)
+        bt = dot2l(split(dot2r(v, ty, ((0,), (1,)))), k)
         pa, pb = split(a), split(b)
         o_ref[i] = near + dot3(qw, pb, NT)
         put(qt_ref, i, split(dot3(qw, pa, NT)))
-        a = a - dot3(pa, rt)
-        b = b + (bt - dot3(pb, rt))
+        a = a - dot3(pa, r, NT)
+        b = b + (bt - dot3(pb, r, NT))
     state_a[...] = a
     state_b[...] = b
 
@@ -211,7 +247,7 @@
 def finish_kernel(o_ref, qt_ref, s_ref, gain_ref, out_ref):
     s = split(s_ref[...])
     for i in range(o_ref.shape[0]):
-        o = o_ref[i] + dot3(get(qt_ref, i), s, NT)
+        o = o_ref[i] + dot3(get(qt_ref, i), s)
         mean = jnp.mean(o * o, axis=1, keepdims=True)
         out_ref[i] = (o * lax.rsqrt(mean + EPS) * gain_ref[...]).astype(BF16)
 
@@ -237,6 +273,13 @@
             out_ref[i, steps:] = rest[0][i]
 
 
+def apart_kernel(me_ref, x_ref, *out_refs):
+    steps, width = out_refs[0].shape
+    for d, out_ref in enumerate(out_refs):
+        at = pl.multiple_of((me_ref[0] ^ d) * width, width)
+        out_ref[...] = x_ref[:, :, pl.ds(at, width)].reshape(steps, width)
+
+
 def rows_kernel(x_ref, out_ref):
     per, _, width = out_ref.shape
     for i in range(per):
@@ -249,13 +292,15 @@
     )
 
 
-def call(kernel, grid, ins, outs, scratch=(), backward=False):
+def in_hbm(x):
+    return pltpu.with_memory_space_constraint(x, pltpu.HBM)
+
+
+def call(kernel, grid, ins, outs, scratch=(), name=None, hbm=True):
     def spec(a, per):
         zeros = (0,) * (len(a.shape) - 1)
         if per is None:
             return pl.BlockSpec(a.shape, lambda c: (0,) + zeros)
-        if backward:
-            return pl.BlockSpec((per,) + a.shape[1:], lambda c: (grid - 1 - c,) + zeros)
         return pl.BlockSpec((per,) + a.shape[1:], lambda c: (c,) + zeros)
 
     return pl.pallas_call(
@@ -263,10 +308,12 @@
         grid=(grid,),
         in_specs=[spec(*i) for i in ins],
         out_specs=[spec(*o) for o in outs],
-        out_shape=[o[0] for o in outs],
+        out_shape=[
+            pltpu.HBM(a.shape, a.dtype) if hbm and per else a for a, per in outs
+        ],
         scratch_shapes=list(scratch),
         compiler_params=params(),
-    )(*[i[0] for i in ins])
+    )(*[in_hbm(a) if name == "local" else a for a, _ in ins])
 
 
 def by_head(x, width, extra=None, per=4):
@@ -291,6 +338,82 @@
     )(*args)
 
 
+SCALAR = pl.BlockSpec(memory_space=pltpu.SMEM)
+WHOLE = pl.BlockSpec(memory_space=pltpu.VMEM)
+
+
+def apart(x, me, count, width):
+    steps = x.shape[0] * x.shape[1]
+    return pl.pallas_call(
+        apart_kernel,
+        in_specs=[SCALAR, WHOLE],
+        out_specs=[WHOLE] * count,
+        out_shape=[jax.ShapeDtypeStruct((steps, width), x.dtype)] * count,
+        name="apart",
+        compiler_params=pltpu.CompilerParams(vmem_limit_bytes=VMEM_LIMIT),
+    )(me, x)
+
+
+def keys_call(k, blocks, steps, width, per):
+    groups = blocks // per
+    hbm = [
+        ((blocks, 2, steps, steps), BF16),
+        ((blocks, 8, steps), F32),
+        ((blocks, 2, width, width), BF16),
+        ((blocks, 2, width, steps), BF16),
+    ]
+
+    def spec(shape, late=0):
+        def at(c):
+            return (jnp.clip(groups - 1 + late - c, 0, groups - 1),) + (0,) * (len(shape) - 1)
+
+        return pl.BlockSpec((per,) + tuple(shape[1:]), at)
+
+    vmem = pltpu.VMEM
+    return pl.pallas_call(
+        keys_kernel,
+        grid=(groups + 1,),
+        in_specs=[spec(k.shape)],
+        out_specs=[spec(s, i == 3) for i, (s, _) in enumerate(hbm)]
+        + [pl.BlockSpec((width, width), lambda c: (0, 0))],
+        out_shape=[pltpu.HBM(*h) for h in hbm] + [jax.ShapeDtypeStruct((width, width), F32)],
+        scratch_shapes=[
+            vmem((width, width), F32),
+            vmem((2, per, steps, width), BF16),
+            vmem((2, per, 2, steps, steps), BF16),
+            vmem((2, per, 2, width, width), BF16),
+            vmem((2, per, 1, steps), F32),
+        ],
+        name="keys",
+        compiler_params=params(),
+    )(k)
+
+
+def ends(me, e, vs, per):
+    steps, width = vs[0].shape
+    sds = jax.ShapeDtypeStruct
+
+    def at(g, me):
+        return (me[0] // per) ^ g
+
+    return pl.pallas_call(
+        functools.partial(ends_kernel, per=per),
+        grid_spec=pltpu.PrefetchScalarGridSpec(
+            num_scalar_prefetch=1,
+            grid=(len(vs) // per,),
+            in_specs=[pl.BlockSpec((per,) + e.shape[1:], lambda g, me: (at(g, me), 0, 0, 0))]
+            + [WHOLE] * len(vs),
+            out_specs=[
+                pl.BlockSpec((per, steps, width), lambda g, me: (at(g, me), 0, 0)),
+                pl.BlockSpec((width, width), lambda g, me: (0, 0)),
+            ],
+        ),
+        out_shape=[pltpu.HBM((len(vs), steps, width), BF16), sds((width, width), F32)],
+        name="ends",
+        compiler_params=params(),
+    )(me, in_hbm(e), *vs)
+
+
 def shards(queries, keys, values, betas, gate, norm_gain):
     toks, refl = keys.shape[:2]
     width = norm_gain.shape[0]
@@ -305,42 +428,34 @@
 
     b_rows = jnp.broadcast_to(betas.reshape(steps, heads).T[:, None, :], (heads, PAD, steps))
     k = exchange(by_head(keys, width, b_rows))
-    v_out, q_out = by_head(values, width), by_head(queries, width, per=8)
-    v = exchange(v_out)
+    me = lax.axis_index(near)[None].astype(jnp.int32)
+    v_parts = apart(values, me, blocks, width)
+    q_out = by_head(queries, width, per=8)
+    vs = [v_parts[0]] + [
+        lax.ppermute(v_parts[d], near, [(i, i ^ d) for i in range(blocks)])
+        for d in range(1, blocks)
+    ]
 
     per = PER_STEP
     grid = blocks // per
     sds = jax.ShapeDtypeStruct
-    square = sds((blocks, 2, width, width), BF16)
-    state = sds((width, width), F32)
     keep = pltpu.VMEM((width, width), F32)
-    t, n, rt, e, end_a = call(
-        keys_kernel,
-        grid,
-        [(k, per)],
-        [
-            (sds((blocks, 2, steps, steps), BF16), per),
-            (sds((blocks, 8, steps), F32), per),
-            (square, per),
-            (sds((blocks, 2, steps, width), BF16), per),
-            (state, None),
-        ],
-        (keep,),
-        backward=True,
-    )
+    t, n, r, e, end_a = keys_call(k, blocks, steps, width, per)
     q = exchange(q_out)
-    (end_b,) = call(ends_kernel, grid, [(v, per), (e, per)], [(state, None)], ())
+    v, end_b = ends(me, e, vs, per)
     route = [(i, i + 1) for i in range(far_size - 1)]
     start = lax.ppermute(end_b, "far", route)
     for _ in range(far_size - 2):
-        sent = jnp.dot(start, end_a, precision=lax.Precision.HIGHEST) + end_b
+        sent = jnp.dot(end_a, start, precision=lax.Precision.HIGHEST) + end_b
         start = lax.ppermute(sent, "far", route)
     o, qt = call(
         local_kernel,
         grid,
-        [(q, per), (k, per), (v, per), (t, per), (n, per), (rt, per)],
+        [(q, per), (k, per), (v, per), (t, per), (n, per), (r, per)],
         [(sds((blocks, toks, width), F32), per), (sds((blocks, 2, toks, width), BF16), per)],
         (keep, keep),
+        "local",
+        hbm=False,
     )
     (normed,) = call(
         finish_kernel,
@@ -348,6 +463,8 @@
         [(o, per), (qt, per), (start, None), (norm_gain[None, :], None)],
         [(sds((blocks, toks, width), BF16), per)],
         (),
+        "finish",
+        hbm=False,
     )
     normed = exchange(normed)
     wide = 4

time: 163 us -> 164 us (level)
  local copies, waits for them, and re-layouts: 18.2 us -> 5.46 us
  starting transfers between devices: 21.2 us -> 31.4 us
  Pallas kernels: 47.9 us -> 53 us
    pallas_call x0 -> x3, Pallas kernels: none -> 30.1 us  [the longest x1 23.9 us: keys_call(): pl.pallas_call(keys_kernel, grid=(groups + 1,), in_specs=[spec(k.shape)],...]
    all_to_all x3 -> x2, waiting for transfers between devices: 53.8 us -> 28.8 us  [exchange(): return lax.all_to_all(x, near, 0, 0, tiled=True)]
    ppermute x0 -> x15, waiting for transfers between devices: none -> 24.3 us  [shards(): lax.ppermute(v_parts[d], near, [(i, i ^ d) for i in range(blocks)])]
    pallas_call x4 -> x2, Pallas kernels: 43.2 us -> 19 us  [call(): pl.pallas_call(kernel, grid=(grid,), in_specs=[spec(*i) for i in ins], ou...]
    ppermute x0 -> x15, starting transfers between devices: none -> 14.8 us  [shards(): lax.ppermute(v_parts[d], near, [(i, i ^ d) for i in range(blocks)])]
    unnamed x35 -> x15, local copies, waits for them, and re-layouts: 18.1 us -> 5.37 us
    all_to_all x3 -> x2, starting transfers between devices: 16.7 us -> 11.9 us  [exchange(): return lax.all_to_all(x, near, 0, 0, tiled=True)]
  transfers between devices with their start and end apart: 4 -> 18, of which waited for: 2 -> 7; matrix products, arithmetic and copies ran while one was open for 0% -> 0% of each run, Pallas kernels for 26% -> 30%
where the time goes in v3:
time: 164 us; the launch traced here: 163 us
  Pallas kernels  53 us (32%)
  waiting for transfers between devices  53 us (32%)
  starting transfers between devices  31.4 us (19%)
  blocking collectives  19.9 us (12%)
  local copies, waits for them, and re-layouts  5.46 us (3%)
    all_to_all x2, waiting for transfers between devices, exchange(): return lax.all_to_all(x, near, 0, 0, tiled=True)  28.8 us
    ppermute x15, waiting for transfers between devices, shards(): lax.ppermute(v_parts[d], near, [(i, i ^ d) for i in range(blocks)])  24.3 us
    pallas_call x1, Pallas kernels, keys_call(): pl.pallas_call(keys_kernel, grid=(groups + 1,), in_specs=[spec(k.shape)],...  23.9 us
    all_to_all x1, blocking collectives, exchange(): return lax.all_to_all(x, near, 0, 0, tiled=True)  19.9 us
    pallas_call x2, Pallas kernels, call(): pl.pallas_call(kernel, grid=(grid,), in_specs=[spec(*i) for i in ins], ou...  19 us
    ppermute x15, starting transfers between devices, shards(): lax.ppermute(v_parts[d], near, [(i, i ^ d) for i in range(blocks)])  14.8 us
    all_to_all x2, starting transfers between devices, exchange(): return lax.all_to_all(x, near, 0, 0, tiled=True)  11.9 us
    unnamed x15, local copies, waits for them, and re-layouts  5.37 us
  transfers between devices with their start and end apart: 18, of which 7 were waited for; matrix products, arithmetic and copies ran while one was open for 0% of the time, Pallas kernels for 30%

profile of v3, /device:TPU:0, one launch (start us, length us, event | category | flops | bytes accessed | tf_op | source)
XLA Modules:
  0.0 163.0 jit_solution(2672743756898607547)
XLA Ops:
  0.9 1.6 copy-done.3
  3.3 1.4 copy-done.1
  4.7 6.4 %all-to-all-start.1 = ((bf16[16,264,256]{2,1,0:T(8,128)(2,1)}), bf16[16,264,256]{2,1,0:T(8,128)(2,1)S(1)}, u32[]{:S(2)}, u32[]{:S(2)}) async-start(bf16[16,264,256]{2,1,0:T(8,128)(2,1)} %copy-done.1), calls=%async_computation.1 | async-start | bytes 4325376 | tf_op jit(solution)/shard_map/all_to_all | solution.py:427
  12.2 28.7 %all-to-all-done.1.k_ref = bf16[16,264,256]{2,1,0:T(8,128)(2,1)S(1)} async-done(((bf16[16,264,256]{2,1,0:T(8,128)(2,1)}), bf16[16,264,256]{2,1,0:T(8,128)(2,1)S(1)}, u32[]{:S(2)}, u32[]{:S(2)}) %all-to-all-start.1) | async-done | bytes 2162720 | tf_op jit(solution)/shard_map/all_to_all | solution.py:427
  41.0 5.4 %all-to-all-start = ((bf16[16,128,256]{2,1,0:T(8,128)(2,1)}), bf16[16,128,256]{2,1,0:T(8,128)(2,1)}, u32[]{:S(2)}, u32[]{:S(2)}) async-start(bf16[16,128,256]{2,1,0:T(8,128)(2,1)} %by_head.2), calls=%async_computation | async-start | bytes 2097152 | tf_op jit(solution)/shard_map/all_to_all | solution.py:427
  46.4 1.6 copy-done.2
  49.5 1.6 %collective-permute-start.1 = (bf16[256,256]{1,0:T(8,128)(2,1)S(1)}, bf16[256,256]{1,0:T(8,128)(2,1)S(1)}, u32[]{:S(2)}, u32[]{:S(2)}) collective-permute-start(bf16[256,256]{1,0:T(8,128)(2,1)S(1)} %get-tuple-element.32), channel_id=1, source_target_pairs={{0,2},{1,3},{2,0},{3,1},{4,6},{5,7},{6,4},{7,5},{8,10},{9,11},{10,... | collective-permute-start | bytes 393224 | tf_op jit(solution)/shard_map/ppermute | solution.py:435
  51.2 1.2 collective-permute-start.10
  52.4 1.5 collective-permute-start.11
  53.8 1.2 collective-permute-start.12
  55.0 2.4 %collective-permute-start.13 = (bf16[256,256]{1,0:T(8,128)(2,1)S(1)}, bf16[256,256]{1,0:T(8,128)(2,1)S(1)}, u32[]{:S(2)}, u32[]{:S(2)}) collective-permute-start(bf16[256,256]{1,0:T(8,128)(2,1)S(1)} %get-tuple-element.44), channel_id=1, source_target_pairs={{0,14},{1,15},{2,12},{3,13},{4,10},{5,11},{6,8},{7,9},{8,6},{9,7},... | collective-permute-start | bytes 393224 | tf_op jit(solution)/shard_map/ppermute | solution.py:435
  57.4 9.7 %collective-permute-done.1.refs_2_ = bf16[256,256]{1,0:T(8,128)(2,1)S(1)} collective-permute-done((bf16[256,256]{1,0:T(8,128)(2,1)S(1)}, bf16[256,256]{1,0:T(8,128)(2,1)S(1)}, u32[]{:S(2)}, u32[]{:S(2)}) %collective-permute-start.1) | collective-permute-done | bytes 131104 | tf_op jit(solution)/shard_map/ppermute | solution.py:435
  67.1 2.1 %collective-permute-start.14 = (bf16[256,256]{1,0:T(8,128)(2,1)S(1)}, bf16[256,256]{1,0:T(8,128)(2,1)S(1)}, u32[]{:S(2)}, u32[]{:S(2)}) collective-permute-start(bf16[256,256]{1,0:T(8,128)(2,1)S(1)} %get-tuple-element.45), channel_id=1, source_target_pairs={{0,15},{1,14},{2,13},{3,12},{4,11},{5,10},{6,9},{7,8},{8,7},{9,6},... | collective-permute-start | bytes 393224 | tf_op jit(solution)/shard_map/ppermute | solution.py:435
  71.6 2.9 %collective-permute-done.13.refs_14_ = bf16[256,256]{1,0:T(8,128)(2,1)S(1)} collective-permute-done((bf16[256,256]{1,0:T(8,128)(2,1)S(1)}, bf16[256,256]{1,0:T(8,128)(2,1)S(1)}, u32[]{:S(2)}, u32[]{:S(2)}) %collective-permute-start.13) | collective-permute-done | bytes 131104 | tf_op jit(solution)/shard_map/ppermute | solution.py:435
  76.8 1.6 collective-permute-done.2.refs_3_
  78.9 6.2 %collective-permute-done.3.refs_4_ = bf16[256,256]{1,0:T(8,128)(2,1)S(1)} collective-permute-done((bf16[256,256]{1,0:T(8,128)(2,1)S(1)}, bf16[256,256]{1,0:T(8,128)(2,1)S(1)}, u32[]{:S(2)}, u32[]{:S(2)}) %collective-permute-start.3) | collective-permute-done | bytes 131104 | tf_op jit(solution)/shard_map/ppermute | solution.py:435
  85.1 2.7 %collective-permute-done.4.refs_5_ = bf16[256,256]{1,0:T(8,128)(2,1)S(1)} collective-permute-done((bf16[256,256]{1,0:T(8,128)(2,1)S(1)}, bf16[256,256]{1,0:T(8,128)(2,1)S(1)}, u32[]{:S(2)}, u32[]{:S(2)}) %collective-permute-start.4) | collective-permute-done | bytes 131104 | tf_op jit(solution)/shard_map/ppermute | solution.py:435
  88.2 23.9 %keys.1 = (bf16[16,2,256,256]{3,2,1,0:T(8,128)(2,1)}, f32[16,8,256]{2,1,0:T(8,128)}, bf16[16,2,256,256]{3,2,1,0:T(8,128)(2,1)}, bf16[16,2,256,256]{3,2,1,0:T(8,128)(2,1)}, f32[256,256]{1,0:T(8,128)}) custom-call(bf16[16,264,256]{2,1,0:T(8,128)(2,1)S(1)} %all-to-all-done.1.k_ref), custom_call_target="tpu_custom_call" | custom-call | tf_op jit(solution)/shard_map/keys/pallas_call | solution.py:373
  112.2 5.1 %ends.1 = (bf16[16,256,256]{2,1,0:T(8,128)(2,1)}, f32[256,256]{1,0:T(8,128)S(1)}) custom-call(s32[1]{0:T(128)} %bitcast.2.me_ref, bf16[16,2,256,256]{3,2,1,0:T(8,128)(2,1)} %get-tuple-element.29.e_ref, bf16[256,256]{1,0:T(8,128)(2,1)S(1)} %get-tuple-element.30.refs_0_, bf16[256,256]{1,0:T(8,128)(2,1)S(1)} %collective-permute-done.refs_1_, ...), custom_call_target="tpu_custom_call" | custom-call | tf_op jit(solution)/shard_map/ends/pallas_call | solution.py:399
  117.3 4.7 %collective-permute-start.15 = (f32[256,256]{1,0:T(8,128)S(1)}, f32[256,256]{1,0:T(8,128)S(1)}, u32[]{:S(2)}, u32[]{:S(2)}) collective-permute-start(f32[256,256]{1,0:T(8,128)S(1)} %get-tuple-element.52), channel_id=1, source_target_pairs={{0,16},{1,17},{2,18},{3,19},{4,20},{5,21},{6,22},{7,23},{8,24},{9,... | collective-permute-start | bytes 786440 | tf_op jit(solution)/shard_map/ppermute | solution.py:447
  122.0 17.0 %shard_map.64 = (f32[16,128,256]{2,1,0:T(8,128)S(1)}, bf16[16,2,128,256]{3,2,1,0:T(8,128)(2,1)S(1)}) custom-call(bf16[16,128,256]{2,1,0:T(8,128)(2,1)} %all-to-all-done.q_ref, bf16[16,264,256]{2,1,0:T(8,128)(2,1)} %copy-done, bf16[16,256,256]{2,1,0:T(8,128)(2,1)} %get-tuple-element.46.v_ref, bf16[16,2,256,256]{3,2,1,0:T(8,128)(2,1)} %get-tuple-element.47.t_ref, ...), custom_call_target="tpu_custom_call" | custom-call | tf_op jit(solution)/shard_map/pallas_call | solution.py:306
  139.1 1.9 %shard_map.65 = bf16[16,128,256]{2,1,0:T(8,128)(2,1)S(1)} custom-call(f32[16,128,256]{2,1,0:T(8,128)S(1)} %get-tuple-element.50.o_ref, bf16[16,2,128,256]{3,2,1,0:T(8,128)(2,1)S(1)} %get-tuple-element.51.qt_ref, f32[256,256]{1,0:T(8,128)S(1)} %collective-permute-done.15.s_ref, f32[1,256]{1,0:T(1,128)S(1)} %bitcast.5), custom_call_target="tpu_custom_call" | custom-call | tf_op jit(solution)/shard_map/pallas_call | solution.py:306
  141.1 19.9 %all_to_all.15.n_ref = bf16[16,128,256]{2,1,0:T(8,128)(2,1)S(1)} all-to-all(bf16[16,128,256]{2,1,0:T(8,128)(2,1)S(1)} %shard_map.65), channel_id=1, replica_groups=mesh['far'=2,'near'=4,'head'=4] {'near','head'}, dimensions={0} | all-to-all | bytes 2097152 | tf_op jit(solution)/shard_map/all_to_all | solution.py:427
  161.0 2.0 %gate.1 = bf16[128,4096]{1,0:T(8,128)(2,1)} custom-call(bf16[16,128,256]{2,1,0:T(8,128)(2,1)S(1)} %all_to_all.15.n_ref, bf16[128,4096]{1,0:T(8,128)(2,1)S(1)} %copy-done.4), custom_call_target="tpu_custom_call" | custom-call | tf_op jit(solution)/shard_map/gate/pallas_call | solution.py:471
  (38 shorter events, 10.0 us)
Async XLA Ops:
  0.9 1.6 copy-start.3
  4.7 6.5 %copy-start.5 = (bf16[128,4096]{1,0:T(8,128)(2,1)S(1)}, bf16[128,4096]{1,0:T(8,128)(2,1)}, u32[]{:S(2)}) copy-start(bf16[128,4096]{1,0:T(8,128)(2,1)} %x_ref.3) | copy-start | bytes 3145732
  4.7 36.3 %all-to-all-start.1 = ((bf16[16,264,256]{2,1,0:T(8,128)(2,1)}), bf16[16,264,256]{2,1,0:T(8,128)(2,1)S(1)}, u32[]{:S(2)}, u32[]{:S(2)}) async-start(bf16[16,264,256]{2,1,0:T(8,128)(2,1)} %copy-done.1), calls=%async_computation.1 | async-start | bytes 4325376 | tf_op jit(solution)/shard_map/all_to_all | solution.py:427
  41.0 71.2 %copy-start = (bf16[16,264,256]{2,1,0:T(8,128)(2,1)}, bf16[16,264,256]{2,1,0:T(8,128)(2,1)S(1)}, u32[]{:S(2)}) copy-start(bf16[16,264,256]{2,1,0:T(8,128)(2,1)S(1)} %all-to-all-done.1.k_ref) | copy-start | bytes 6488068
  41.0 81.0 %all-to-all-start = ((bf16[16,128,256]{2,1,0:T(8,128)(2,1)}), bf16[16,128,256]{2,1,0:T(8,128)(2,1)}, u32[]{:S(2)}, u32[]{:S(2)}) async-start(bf16[16,128,256]{2,1,0:T(8,128)(2,1)} %by_head.2), calls=%async_computation | async-start | bytes 2097152 | tf_op jit(solution)/shard_map/all_to_all | solution.py:427
  46.4 1.6 copy-start.2
  49.1 5.9 %collective-permute-start = (bf16[256,256]{1,0:T(8,128)(2,1)S(1)}, bf16[256,256]{1,0:T(8,128)(2,1)S(1)}, u32[]{:S(2)}, u32[]{:S(2)}) collective-permute-start(bf16[256,256]{1,0:T(8,128)(2,1)S(1)} %get-tuple-element.31), channel_id=1, source_target_pairs={{0,1},{1,0},{2,3},{3,2},{4,5},{5,4},{6,7},{7,6},{8,9},{9,8},{10,11... | collective-permute-start | bytes 393224 | tf_op jit(solution)/shard_map/ppermute | solution.py:435
  49.5 17.6 %collective-permute-start.1 = (bf16[256,256]{1,0:T(8,128)(2,1)S(1)}, bf16[256,256]{1,0:T(8,128)(2,1)S(1)}, u32[]{:S(2)}, u32[]{:S(2)}) collective-permute-start(bf16[256,256]{1,0:T(8,128)(2,1)S(1)} %get-tuple-element.32), channel_id=1, source_target_pairs={{0,2},{1,3},{2,0},{3,1},{4,6},{5,7},{6,4},{7,5},{8,10},{9,11},{10,... | collective-permute-start | bytes 393224 | tf_op jit(solution)/shard_map/ppermute | solution.py:435
  51.2 18.0 %collective-permute-start.10 = (bf16[256,256]{1,0:T(8,128)(2,1)S(1)}, bf16[256,256]{1,0:T(8,128)(2,1)S(1)}, u32[]{:S(2)}, u32[]{:S(2)}) collective-permute-start(bf16[256,256]{1,0:T(8,128)(2,1)S(1)} %get-tuple-element.41), channel_id=1, source_target_pairs={{0,11},{1,10},{2,9},{3,8},{4,15},{5,14},{6,13},{7,12},{8,3},{9,2},... | collective-permute-start | bytes 393224 | tf_op jit(solution)/shard_map/ppermute | solution.py:435
  52.4 17.6 %collective-permute-start.11 = (bf16[256,256]{1,0:T(8,128)(2,1)S(1)}, bf16[256,256]{1,0:T(8,128)(2,1)S(1)}, u32[]{:S(2)}, u32[]{:S(2)}) collective-permute-start(bf16[256,256]{1,0:T(8,128)(2,1)S(1)} %get-tuple-element.42), channel_id=1, source_target_pairs={{0,12},{1,13},{2,14},{3,15},{4,8},{5,9},{6,10},{7,11},{8,4},{9,5},... | collective-permute-start | bytes 393224 | tf_op jit(solution)/shard_map/ppermute | solution.py:435
  53.8 17.1 %collective-permute-start.12 = (bf16[256,256]{1,0:T(8,128)(2,1)S(1)}, bf16[256,256]{1,0:T(8,128)(2,1)S(1)}, u32[]{:S(2)}, u32[]{:S(2)}) collective-permute-start(bf16[256,256]{1,0:T(8,128)(2,1)S(1)} %get-tuple-element.43), channel_id=1, source_target_pairs={{0,13},{1,12},{2,15},{3,14},{4,9},{5,8},{6,11},{7,10},{8,5},{9,4},... | collective-permute-start | bytes 393224 | tf_op jit(solution)/shard_map/ppermute | solution.py:435
  55.0 19.5 %collective-permute-start.13 = (bf16[256,256]{1,0:T(8,128)(2,1)S(1)}, bf16[256,256]{1,0:T(8,128)(2,1)S(1)}, u32[]{:S(2)}, u32[]{:S(2)}) collective-permute-start(bf16[256,256]{1,0:T(8,128)(2,1)S(1)} %get-tuple-element.44), channel_id=1, source_target_pairs={{0,14},{1,15},{2,12},{3,13},{4,10},{5,11},{6,8},{7,9},{8,6},{9,7},... | collective-permute-start | bytes 393224 | tf_op jit(solution)/shard_map/ppermute | solution.py:435
  67.1 9.1 %collective-permute-start.14 = (bf16[256,256]{1,0:T(8,128)(2,1)S(1)}, bf16[256,256]{1,0:T(8,128)(2,1)S(1)}, u32[]{:S(2)}, u32[]{:S(2)}) collective-permute-start(bf16[256,256]{1,0:T(8,128)(2,1)S(1)} %get-tuple-element.45), channel_id=1, source_target_pairs={{0,15},{1,14},{2,13},{3,12},{4,11},{5,10},{6,9},{7,8},{8,7},{9,6},... | collective-permute-start | bytes 393224 | tf_op jit(solution)/shard_map/ppermute | solution.py:435
  69.2 9.2 %collective-permute-start.2 = (bf16[256,256]{1,0:T(8,128)(2,1)S(1)}, bf16[256,256]{1,0:T(8,128)(2,1)S(1)}, u32[]{:S(2)}, u32[]{:S(2)}) collective-permute-start(bf16[256,256]{1,0:T(8,128)(2,1)S(1)} %get-tuple-element.33), channel_id=1, source_target_pairs={{0,3},{1,2},{2,1},{3,0},{4,7},{5,6},{6,5},{7,4},{8,11},{9,10},{10,... | collective-permute-start | bytes 393224 | tf_op jit(solution)/shard_map/ppermute | solution.py:435
  69.9 15.2 %collective-permute-start.3 = (bf16[256,256]{1,0:T(8,128)(2,1)S(1)}, bf16[256,256]{1,0:T(8,128)(2,1)S(1)}, u32[]{:S(2)}, u32[]{:S(2)}) collective-permute-start(bf16[256,256]{1,0:T(8,128)(2,1)S(1)} %get-tuple-element.34), channel_id=1, source_target_pairs={{0,4},{1,5},{2,6},{3,7},{4,0},{5,1},{6,2},{7,3},{8,12},{9,13},{10,... | collective-permute-start | bytes 393224 | tf_op jit(solution)/shard_map/ppermute | solution.py:435
  70.9 16.9 %collective-permute-start.4 = (bf16[256,256]{1,0:T(8,128)(2,1)S(1)}, bf16[256,256]{1,0:T(8,128)(2,1)S(1)}, u32[]{:S(2)}, u32[]{:S(2)}) collective-permute-start(bf16[256,256]{1,0:T(8,128)(2,1)S(1)} %get-tuple-element.35), channel_id=1, source_target_pairs={{0,5},{1,4},{2,7},{3,6},{4,1},{5,0},{6,3},{7,2},{8,13},{9,12},{10,... | collective-permute-start | bytes 393224 | tf_op jit(solution)/shard_map/ppermute | solution.py:435
  74.5 37.7 %collective-permute-start.5 = (bf16[256,256]{1,0:T(8,128)(2,1)S(1)}, bf16[256,256]{1,0:T(8,128)(2,1)S(1)}, u32[]{:S(2)}, u32[]{:S(2)}) collective-permute-start(bf16[256,256]{1,0:T(8,128)(2,1)S(1)} %get-tuple-element.36), channel_id=1, source_target_pairs={{0,6},{1,7},{2,4},{3,5},{4,2},{5,3},{6,0},{7,1},{8,14},{9,15},{10,... | collective-permute-start | bytes 393224 | tf_op jit(solution)/shard_map/ppermute | solution.py:435
  76.2 36.0 %collective-permute-start.6 = (bf16[256,256]{1,0:T(8,128)(2,1)S(1)}, bf16[256,256]{1,0:T(8,128)(2,1)S(1)}, u32[]{:S(2)}, u32[]{:S(2)}) collective-permute-start(bf16[256,256]{1,0:T(8,128)(2,1)S(1)} %get-tuple-element.37), channel_id=1, source_target_pairs={{0,7},{1,6},{2,5},{3,4},{4,3},{5,2},{6,1},{7,0},{8,15},{9,14},{10,... | collective-permute-start | bytes 393224 | tf_op jit(solution)/shard_map/ppermute | solution.py:435
  78.4 33.8 %collective-permute-start.7 = (bf16[256,256]{1,0:T(8,128)(2,1)S(1)}, bf16[256,256]{1,0:T(8,128)(2,1)S(1)}, u32[]{:S(2)}, u32[]{:S(2)}) collective-permute-start(bf16[256,256]{1,0:T(8,128)(2,1)S(1)} %get-tuple-element.38), channel_id=1, source_target_pairs={{0,8},{1,9},{2,10},{3,11},{4,12},{5,13},{6,14},{7,15},{8,0},{9,1},... | collective-permute-start | bytes 393224 | tf_op jit(solution)/shard_map/ppermute | solution.py:435
  85.1 27.1 %collective-permute-start.8 = (bf16[256,256]{1,0:T(8,128)(2,1)S(1)}, bf16[256,256]{1,0:T(8,128)(2,1)S(1)}, u32[]{:S(2)}, u32[]{:S(2)}) collective-permute-start(bf16[256,256]{1,0:T(8,128)(2,1)S(1)} %get-tuple-element.39), channel_id=1, source_target_pairs={{0,9},{1,8},{2,11},{3,10},{4,13},{5,12},{6,15},{7,14},{8,1},{9,0},... | collective-permute-start | bytes 393224 | tf_op jit(solution)/shard_map/ppermute | solution.py:435
  87.8 24.4 %collective-permute-start.9 = (bf16[256,256]{1,0:T(8,128)(2,1)S(1)}, bf16[256,256]{1,0:T(8,128)(2,1)S(1)}, u32[]{:S(2)}, u32[]{:S(2)}) collective-permute-start(bf16[256,256]{1,0:T(8,128)(2,1)S(1)} %get-tuple-element.40), channel_id=1, source_target_pairs={{0,10},{1,11},{2,8},{3,9},{4,14},{5,15},{6,12},{7,13},{8,2},{9,3},... | collective-permute-start | bytes 393224 | tf_op jit(solution)/shard_map/ppermute | solution.py:435
  117.3 21.8 %collective-permute-start.15 = (f32[256,256]{1,0:T(8,128)S(1)}, f32[256,256]{1,0:T(8,128)S(1)}, u32[]{:S(2)}, u32[]{:S(2)}) collective-permute-start(f32[256,256]{1,0:T(8,128)S(1)} %get-tuple-element.52), channel_id=1, source_target_pairs={{0,16},{1,17},{2,18},{3,19},{4,20},{5,21},{6,22},{7,23},{8,24},{9,... | collective-permute-start | bytes 786440 | tf_op jit(solution)/shard_map/ppermute | solution.py:447
  122.0 17.1 %copy-start.6 = (f32[256]{0:T(256)S(1)}, f32[256]{0:T(256)}, u32[]{:S(2)}) copy-start(f32[256]{0:T(256)} %param.11) | copy-start | bytes 3076
  141.0 20.0 %copy-start.4 = (bf16[128,4096]{1,0:T(8,128)(2,1)S(1)}, bf16[128,4096]{1,0:T(8,128)(2,1)}, u32[]{:S(2)}) copy-start(bf16[128,4096]{1,0:T(8,128)(2,1)} %gate_ref.1) | copy-start | bytes 3145732
  (1 other events, 1.4 us)
